TPU v7x, 512 devices: a whole 4x4x16 slice. The times are simulated.
512 devices in a mesh: band: 64 (over z, x), disp: 8 (over y, core).
Axes of the slice: x: 4, y: 4, z: 16, core: 2. Of those that a mesh axis runs over, the one named last changes fastest.
Arguments:
- feat_left: bfloat16 [64, 96, 1024], P('band', None, 'disp'), may hold values from -19 to 19
- feat_right: bfloat16 [64, 96, 1024], P('band', None, 'disp'), may hold values from -19 to 19
- limit: int32 [64, 1024], P('band', 'disp'), may hold values from 24 to 96
- indices: int32 [3, 64, 1024], P(None, 'band', 'disp'), may hold values from 0 to 95
- hidden_start: bfloat16 [64, 1024, 128], P('band', 'disp'), may hold values from -1 to 1
- vol_kernel: bfloat16 [3, 3, 3, 8, 8], replicated, may hold values from -0.4375 to 0.4375
- group_gain: float32 [8], replicated, may hold values from 0.5 to 2
- hid_kernel: bfloat16 [3, 3, 128, 384], replicated, may hold values from -0.1875 to 0.1875
- in_kernel: bfloat16 [3, 3, 9, 384], replicated, may hold values from -0.625 to 0.625
- head_weight: bfloat16 [128, 1], replicated, may hold values from -0.5 to 0.5
Outputs:
- disparity: float32 [64, 1024], P('band', 'disp')
- hidden: bfloat16 [64, 1024, 128], P('band', 'disp')
All inputs are finite; a program needn't handle non-finite values.
Results may differ from a plain program's by a relative error of at most 0.007.
Values may be sent and summed in bfloat16 or wider, within the bound.
A program may use at most 128 MiB of HBM per device.

v0:
```python
import jax
import jax.numpy as jnp
from jax import lax
from jax.experimental import pallas as pl
from jax.experimental.pallas import tpu as pltpu
from jax.sharding import PartitionSpec as P

GROUPS = 8
DISPS = 96
PER_GROUP = 12
CH = 96
HID = 128
ITERS = 3
COLS = 128

MESH = pl.DeviceIdType.MESH
F32 = jnp.float32
BF16 = jnp.bfloat16

AROUND = [(r, c) for r in range(-2, 3) for c in (-1, 0, 1) if (r, c) != (0, 0)]
BLOCK = 14
PAIRS = 50
EXT = COLS + 16
NT = (((1,), (1,)), ((), ()))


def dot(a, b):
    return jnp.dot(a, b, preferred_element_type=F32)


def dot_nt(a, b):
    return lax.dot_general(a, b, NT, preferred_element_type=F32)


def iota(shape, dim):
    return lax.broadcasted_iota(jnp.int32, shape, dim)


def one_hot(cond):
    return jnp.where(cond, 1.0, 0.0).astype(BF16)


def kernel(
    gain_ref, fl_in, fr_in, lim_in, ind_in, h0_in, vk_in, hk_in, ik_in, hw_in,
    disp_out, hid_out,
    fl, fr, fp, edge, edge_l, edge_r, lim, ind, vk, ik, hw,
    lp, rc, rp, el, er, ins, tw, lg,
    hr, hl, hrt, lm, hf, rf, dd, lk3, x4, xr, w4, win, ikf,
    local_sem, feat_send, feat_recv, hid_send, hid_recv, look_send, look_recv,
):
    band, disp = lax.axis_index("band"), lax.axis_index("disp")
    bands, disps = lax.axis_size("band"), lax.axis_size("disp")

    def device(r, c):
        return (lax.rem(band + r + bands, bands), lax.rem(disp + c + disps, disps))

    locals_ = [
        pltpu.make_async_copy(src, dst, local_sem.at[i])
        for i, (src, dst) in enumerate(
            [
                (fl_in, fl.at[1]),
                (fr_in, fr.at[1]),
                (vk_in, vk),
                (ik_in, ik),
                (hw_in, hw),
                (lim_in, lim),
                (ind_in, ind),
                (h0_in, hr.at[0, 2]),
                (hk_in, w4.at[:, 0:384, :]),
            ]
        )
    ]
    for copy in locals_:
        copy.start()

    barrier = pltpu.get_barrier_semaphore()
    for r, c in AROUND:
        pl.semaphore_signal(barrier, inc=1, device_id=device(r, c), device_id_type=MESH)

    locals_[0].wait()
    locals_[1].wait()
    pad = jnp.zeros((32, COLS), BF16)
    row16, lane16 = iota((16, COLS), 0), iota((16, COLS), 1)
    pick_left = one_hot(((row16 == 0) & (lane16 == 0)) | ((row16 == 2) & (lane16 == COLS - 1)))
    pick_right = one_hot((row16 == 1) & (lane16 == 0))
    edge[...] = (
        dot_nt(pick_left, jnp.concatenate([fl[1], pad], 0))
        + dot_nt(pick_right, jnp.concatenate([fr[1], pad], 0))
    ).astype(BF16)

    pl.semaphore_wait(barrier, len(AROUND))

    def remote(src, dst, send, recv, i, r, c):
        return pltpu.make_async_remote_copy(
            src_ref=src, dst_ref=dst, send_sem=send.at[i], recv_sem=recv.at[i],
            device_id=device(r, c), device_id_type=MESH,
        )

    feats = {}
    plan = [(r, -1, "p") for r in (0, -1, 1)] + [(r, -1, "e") for r in (0, -1, 1)]
    plan += [(r, 1, "e") for r in (0, -1, 1)]
    plan += [(r, 0, kind) for r in (-1, 1) for kind in ("l", "r")]
    for i, (r, c, kind) in enumerate(plan):
        src, dst = {
            "p": (fr_in, fp.at[r + 1]),
            "e": (edge, (edge_l if c < 0 else edge_r).at[r + 1]),
            "l": (fl_in, fl.at[r + 1]),
            "r": (fr_in, fr.at[r + 1]),
        }[kind]
        feats[(r, c, kind)] = remote(src, dst, feat_send, feat_recv, i, -r, -c)
        feats[(r, c, kind)].start()

    def hidden_copies(t):
        copies = []
        for i, (r, c) in enumerate(AROUND):
            own = h0_in if t == 0 else hr.at[t, 2]
            if c == 0:
                src, dst = own, hr.at[t, r + 2]
            elif c < 0:
                src, dst = own.at[COLS - 16 : COLS], hl.at[t, r + 2]
            else:
                src, dst = own.at[0:16], hrt.at[t, r + 2]
            copies.append(
                remote(src, dst, hid_send.at[t], hid_recv.at[t], i, -r, -c)
            )
        return copies

    hidden_sent = [hidden_copies(0)]
    for copy in hidden_sent[0]:
        copy.start()

    for copy in locals_[2:]:
        copy.wait()
    lane8 = iota((8, COLS), 1)
    spread = one_hot(iota((8, COLS), 0) == lax.rem(lane8, 8))
    taps = dot(vk[...], spread)
    lane_disp = lane8 // 8
    eye = one_hot(iota((128, 128), 0) == iota((128, 128), 1))
    for b in range(3):
        for e in range(3):
            tap = [taps[((a * 3 + b) * 3 + e) * 8 :][:8] for a in range(3)]
            rows = []
            for at in range(16):
                block = jnp.zeros((8, COLS), F32)
                for a in range(3):
                    block = jnp.where(lane_disp == at - a, tap[a], block)
                rows.append(block)
            toeplitz = jnp.concatenate(rows, 0).astype(BF16)
            slot = (b * 3 + e) * 128
            tw[:, slot : slot + 128] = dot_nt(eye, toeplitz).astype(BF16)

    head_rows = jnp.broadcast_to(hw[...].astype(F32), (128, HID)).astype(BF16)
    head = dot_nt(eye, head_rows).astype(BF16)
    head_row = head_rows[0:16]

    ikf[...] = jnp.zeros_like(ikf)
    for a in range(3):
        for i in range(GROUPS + 1):
            ikf[a, 3 * i : 3 * i + 3, :] = ik[a, i].astype(F32)
    source = iota((128, 32), 1)
    source_i, source_b = source // 3, lax.rem(source, 3)
    for t in range(ITERS):
        goes_to = 32 * source_b + jnp.where(source_i < GROUPS, 8 * t + source_i, 24)
        move = one_hot((source < 27) & (iota((128, 32), 0) == goes_to))
        for a in range(3):
            win[t, a] = dot(move, ikf[a].astype(BF16)).astype(BF16)

    hf[...] = jnp.zeros_like(hf)
    rf[...] = jnp.zeros_like(rf)
    dd[...] = jnp.zeros_like(dd)

    row_ok = {r: (band + r >= 0) & (band + r < bands) for r in range(-2, 3)}
    left_ok, right_ok = disp > 0, disp < disps - 1

    def flag(ok):
        return jnp.where(ok, 1.0, 0.0).astype(F32)

    chan = iota((CH, 128), 0)
    perm = one_hot(iota((CH, 128), 1) == lax.rem(chan, 8) * PER_GROUP + chan // 8)
    perm_ch = one_hot(
        iota((CH, CH), 1) == lax.rem(iota((CH, CH), 0), 8) * PER_GROUP + iota((CH, CH), 0) // 8
    )

    def prepare(b):
        lp[b] = dot(perm_ch, fl[b])
        rc[b] = dot(perm_ch, fr[b])
        rp[b] = dot(perm_ch, fp[b]) * flag(left_ok)

        def column(ref, row):
            line = ref[b].astype(F32)[row : row + 1]
            return dot_nt(perm, jnp.broadcast_to(line, (128, 128)).astype(BF16))

        left_col, right_col, right_right = column(edge_l, 2), column(edge_r, 0), column(edge_r, 1)
        left_sum = jnp.zeros((8, COLS), F32)
        right_sum = jnp.zeros((8, COLS), F32)
        for c in range(PER_GROUP):
            s = slice(8 * c, 8 * c + 8)
            left_sum += left_col[s] * rp[b, s]
            right_sum += right_col[s] * jnp.where(lane8 == 0, right_right[s], rc[b, s])
        el[b] = left_sum
        er[b] = right_sum * flag(right_ok)

    scale = [flag(row_ok[r]) * (1.0 / PER_GROUP) for r in (-1, 0, 1)]

    def correlate(rows):
        def pair(k, carry):
            for b in rows:
                found = ([], [], [])
                for u in range(2):
                    d = 2 * k - 1 + u
                    turn = jnp.maximum(d, 0)
                    factor = jnp.where((d >= 0) & (d < DISPS), scale[b], 0.0)
                    keep = lane8 < COLS - turn
                    total = jnp.zeros((8, COLS), F32)
                    for c in range(PER_GROUP):
                        s = slice(8 * c, 8 * c + 8)
                        mixed = jnp.where(keep, rc[b, s], rp[b, s])
                        total += pltpu.roll(mixed, turn, 1) * lp[b, s]
                    raw = total * factor
                    left = pltpu.roll(el[b], turn, 1) * factor
                    right = pltpu.roll(er[b], turn, 1) * factor
                    found[0].append(pltpu.roll(jnp.where(lane8 == COLS - 1, left, raw), 1, 1))
                    found[1].append(raw)
                    found[2].append(pltpu.roll(jnp.where(lane8 == 0, right, raw), COLS - 1, 1))
                at = pl.multiple_of(16 * k, 16)
                for e in range(3):
                    ins[b, e, pl.ds(at, 16), :] = jnp.concatenate(found[e], 0).astype(BF16)
            return carry

        lax.fori_loop(0, PAIRS, pair, 0)

    for key in [(0, -1, "p"), (0, -1, "e"), (0, 1, "e")]:
        feats[key].wait_recv()
    prepare(1)
    correlate([1])
    for key in feats:
        if key[0] != 0:
            feats[key].wait_recv()
    prepare(0)
    prepare(2)
    correlate([0, 2])

    gain = jnp.zeros((8, COLS), F32)
    for g in range(GROUPS):
        gain = jnp.where(iota((8, COLS), 0) == g, gain_ref[g], gain)
    at_disp = [jnp.broadcast_to(ind[t], (8, COLS)) for t in range(ITERS)]
    looked = [jnp.zeros((8, COLS), F32) for _ in range(ITERS)]
    for j in range(7):
        first = BLOCK * 8 * j
        windows = [ins[b, e, first : first + 128, :] for b in range(3) for e in range(3)]
        conv = dot(tw[0 : BLOCK * 8, :], jnp.concatenate(windows, 0))
        raw = windows[4].astype(F32)[8 : 8 + BLOCK * 8]
        volume = (raw + jnp.maximum(conv, 0.0)).astype(BF16).astype(F32)
        volume = volume.reshape(BLOCK, 8, COLS)
        count = min(BLOCK, DISPS - BLOCK * j)
        lg[BLOCK * j : BLOCK * j + BLOCK, :] = jnp.sum(volume * gain[None], axis=1)
        for q in range(count):
            for t in range(ITERS):
                looked[t] = jnp.where(at_disp[t] == BLOCK * j + q, volume[q], looked[t])

    levels = iota((DISPS, COLS), 0)
    valid = levels < lim[...]
    masked = jnp.where(valid, lg[0:DISPS, :], -1e30)
    weights = jnp.where(valid, jnp.exp(masked - jnp.max(masked, axis=0, keepdims=True)), 0.0)
    moment = jnp.sum(weights * levels.astype(F32), axis=0, keepdims=True)
    disparity = moment / jnp.sum(weights, axis=0, keepdims=True) / 8.0

    high = disparity.astype(BF16).astype(F32)
    middle = (disparity - high).astype(BF16).astype(F32)
    low = disparity - high - middle
    sub8 = iota((8, COLS), 0)
    parts = jnp.zeros((8, COLS), F32)
    for i, part in enumerate((high, middle, low)):
        parts = jnp.where(sub8 == i, part, parts)
    lm[2, 1] = jnp.concatenate(looked + [parts], 0).astype(BF16)
    look_copies = [
        remote(lm.at[2, 1], lm.at[r + 2, c + 1], look_send, look_recv, i, -r, -c)
        for i, (r, c) in enumerate(AROUND)
    ]
    for copy in look_copies:
        copy.start()
    for copy in look_copies:
        copy.wait_recv()

    lane32 = iota((32, COLS), 1)
    place = one_hot(iota((EXT, 256), 0) == iota((EXT, 256), 1))
    take = one_hot((iota((128, 128), 0) >= 56) & (iota((128, 128), 0) < 59))
    for r in range(-2, 3):
        def tile(c, ok):
            return jnp.where(ok, lm[r + 2, c + 1].astype(F32), 0.0)

        left, own, right = (
            tile(-1, row_ok[r] & left_ok), tile(0, row_ok[r]), tile(1, row_ok[r] & right_ok)
        )
        lows, highs = [], []
        for s in (-1, 0, 1):
            lows.append(pltpu.roll(jnp.where(lane32 < 120 + s, own, left), 8 - s, 1))
            highs.append(pltpu.roll(jnp.where(lane32 < 120 + s, right, own), 8 - s, 1))
        zero = jnp.zeros((32, COLS), F32)
        wide = jnp.concatenate(
            [jnp.concatenate(lows + [zero], 0), jnp.concatenate(highs + [zero], 0)], 1
        ).astype(BF16)
        found = dot_nt(place, wide)
        lk3[r + 2] = found
        dd[r + 2, 8 : 8 + EXT, :] = dot(found.astype(BF16), take)

    lane_ext = iota((EXT, 128), 1)
    for t in range(ITERS):
        for copy in hidden_sent[t]:
            copy.wait_recv()
        for r in range(-2, 3):
            i = r + 2
            own = jnp.where(row_ok[r], hr[t, i].astype(F32), 0.0)
            left = jnp.where(row_ok[r] & left_ok, hl[t, i].astype(F32), 0.0)
            right = jnp.where(row_ok[r] & right_ok, hrt[t, i].astype(F32), 0.0)
            hf[i, 16 : 16 + COLS, :] = own
            hf[i, 8:16, :] = left[8:16]
            hf[i, 16 + COLS : 24 + COLS, :] = right[0:8]
            for b in range(3):
                x4[i, :, 128 * b : 128 * b + 128] = hf[i, 7 + b : 7 + b + EXT, :].astype(BF16)
            if t > 0:
                dd[i, 8 : 8 + EXT, :] += dot(x4[i, :, 128:256], head)
            inputs = lk3[i]
            for b in range(3):
                shifted = 0.25 * dd[i, 7 + b : 7 + b + EXT, :]
                inputs = jnp.where(lane_ext == 32 * b + 24, shifted, inputs)
            x4[i, :, 384:512] = inputs.astype(BF16)
        for a in range(3):
            w4[a, 384:512, :] = win[t, a]
        gates = jnp.zeros((3 * EXT, 256), F32)
        for a in range(3):
            gates += dot(x4[a : a + 3].reshape(3 * EXT, 512), w4[a, :, 0:256])
        update = jax.nn.sigmoid(gates[EXT : 2 * EXT, 0:128])
        reset = jax.nn.sigmoid(gates[:, 128:256]).reshape(3, EXT, 128)
        rf[:, 8 : 8 + EXT, :] = reset * hf[1:4, 8 : 8 + EXT, :]
        pre = jnp.zeros((EXT, 128), F32)
        for a in range(3):
            for b in range(3):
                xr[:, 128 * b : 128 * b + 128] = rf[a, 7 + b : 7 + b + EXT, :].astype(BF16)
            xr[:, 384:512] = x4[a + 1, :, 384:512]
            pre += dot(xr[...], w4[a, :, 256:384])
        candidate = jnp.tanh(pre)
        fresh = (1.0 - update) * hf[2, 8 : 8 + EXT, :] + update * candidate
        fresh = fresh[8 : 8 + COLS].astype(BF16)
        disparity += dot_nt(head_row, fresh)[0:1]
        if t < ITERS - 1:
            hr[t + 1, 2] = fresh
            hidden_sent.append(hidden_copies(t + 1))
            for copy in hidden_sent[t + 1]:
                copy.start()
        else:
            hid_out[...] = fresh
    disp_out[...] = disparity

    for copy in list(feats.values()) + look_copies + sum(hidden_sent, []):
        copy.wait_send()


def local(
    feat_left, feat_right, limit, indices, hidden_start,
    vol_kernel, group_gain, hid_kernel, in_kernel, head_weight,
):
    any_spec = pl.BlockSpec(memory_space=pl.ANY)
    vmem = pl.BlockSpec(memory_space=pltpu.VMEM)
    dma = pltpu.SemaphoreType.DMA
    disparity, hidden = pl.pallas_call(
        kernel,
        out_shape=(
            jax.ShapeDtypeStruct((1, COLS), F32),
            jax.ShapeDtypeStruct((COLS, HID), BF16),
        ),
        in_specs=[pl.BlockSpec(memory_space=pltpu.SMEM)] + [any_spec] * 9,
        out_specs=(vmem, vmem),
        scratch_shapes=[
            pltpu.VMEM((3, CH, COLS), BF16),
            pltpu.VMEM((3, CH, COLS), BF16),
            pltpu.VMEM((3, CH, COLS), BF16),
            pltpu.VMEM((16, 128), BF16),
            pltpu.VMEM((3, 16, 128), BF16),
            pltpu.VMEM((3, 16, 128), BF16),
            pltpu.VMEM((1, COLS), jnp.int32),
            pltpu.VMEM((ITERS, 1, COLS), jnp.int32),
            pltpu.VMEM((216, 8), BF16),
            pltpu.VMEM((3, 9, 3, 384), BF16),
            pltpu.VMEM((1, HID), BF16),
            pltpu.VMEM((3, CH, COLS), F32),
            pltpu.VMEM((3, CH, COLS), F32),
            pltpu.VMEM((3, CH, COLS), F32),
            pltpu.VMEM((3, 8, COLS), F32),
            pltpu.VMEM((3, 8, COLS), F32),
            pltpu.VMEM((3, 3, PAIRS * 16, COLS), BF16),
            pltpu.VMEM((128, 9 * 128), BF16),
            pltpu.VMEM((104, COLS), F32),
            pltpu.VMEM((ITERS, 5, COLS, HID), BF16),
            pltpu.VMEM((ITERS, 5, 16, HID), BF16),
            pltpu.VMEM((ITERS, 5, 16, HID), BF16),
            pltpu.VMEM((5, 3, 32, COLS), BF16),
            pltpu.VMEM((5, EXT + 16, 128), F32),
            pltpu.VMEM((3, EXT + 16, 128), F32),
            pltpu.VMEM((5, EXT + 16, 128), F32),
            pltpu.VMEM((5, EXT, 128), F32),
            pltpu.VMEM((5, EXT, 512), BF16),
            pltpu.VMEM((EXT, 512), BF16),
            pltpu.VMEM((3, 512, 384), BF16),
            pltpu.VMEM((ITERS, 3, 128, 384), BF16),
            pltpu.VMEM((3, 32, 384), F32),
            dma((9,)),
            dma((13,)),
            dma((13,)),
            dma((ITERS, len(AROUND))),
            dma((ITERS, len(AROUND))),
            dma((len(AROUND),)),
            dma((len(AROUND),)),
        ],
        compiler_params=pltpu.CompilerParams(collective_id=0, has_side_effects=True),
        name="stereo",
    )(
        group_gain,
        feat_left[0],
        feat_right[0],
        limit,
        indices,
        hidden_start[0],
        vol_kernel.reshape(216, 8),
        hid_kernel.reshape(3, 384, 384),
        in_kernel.transpose(0, 2, 1, 3),
        head_weight.reshape(1, HID),
    )
    return disparity, hidden[None]


def solution(mesh):
    in_specs = (
        P("band", None, "disp"),
        P("band", None, "disp"),
        P("band", "disp"),
        P(None, "band", "disp"),
        P("band", "disp", None),
        P(),
        P(),
        P(),
        P(),
        P(),
    )
    out_specs = (P("band", "disp"), P("band", "disp", None))
    return jax.shard_map(local, mesh=mesh, in_specs=in_specs, out_specs=out_specs, check_vma=False)
```

profile of v0, /device:TPU:1, one launch (start us, length us, event | category | flops | bytes accessed | tf_op | source)
XLA Modules:
  0.0 63.6 jit_solution(9104777022253746873)
XLA Ops:
  0.6 60.5 %stereo.1 = (f32[1,128]{1,0:T(1,128)}, bf16[128,128]{1,0:T(8,128)(2,1)}) custom-call(f32[8]{0:T(128)} %gain_ref.1, bf16[96,128]{1,0:T(8,128)(2,1)} %bitcast.13, bf16[96,128]{1,0:T(8,128)(2,1)} %bitcast.14, s32[1,128]{1,0:T(1,128)} %lim_in.1, s32[3,1,128]{2,1,0:T(1,128)} %ind_in.1, bf16[128,128]{1,0:T(8,128)(2,1)} %bitcast.11, bf16[216,8]{1,0:T(8,128)(2,1)} %bitcast.10, ...), custom_call_target="tpu_custom_call" | custom-call | tf_op jit(solution)/shard_map/stereo/pallas_call | solution.py:366
  61.1 0.0 copy-start
  61.1 0.6 copy-done
  61.7 0.5 copy.14
  62.3 1.4 %copy.15 = bf16[1,128,128]{2,1,0:T(8,128)(2,1)} copy(bf16[1,128,128]{2,1,0:T(8,128)(2,1)} %bitcast.12) | data formatting | bytes 65536
Async XLA Ops:
  61.1 0.6 copy-start
where the time goes:
time: 63.9 us; the launch traced here: 63.6 us
  Pallas kernels  60.5 us (95%)
  local copies, waits for them, and re-layouts  2.51 us (4%)
  between operations  0.65 us (1%)
    pallas_call x1, Pallas kernels, local(): pl.pallas_call(kernel, out_shape=(jax.ShapeDtypeStruct((1, COLS), F32), j...  60.5 us
    unnamed x4, local copies, waits for them, and re-layouts  2.51 us

commit v1 on v0

--- a/solution.py
+++ b/solution.py
@@ -18,8 +18,8 @@
 BF16 = jnp.bfloat16
 
 AROUND = [(r, c) for r in range(-2, 3) for c in (-1, 0, 1) if (r, c) != (0, 0)]
-BLOCK = 14
-PAIRS = 50
+BLOCK = 16
+WINDOW = 8 * (BLOCK + 2)
 EXT = COLS + 16
 NT = (((1,), (1,)), ((), ()))
 
@@ -44,7 +44,7 @@
     gain_ref, fl_in, fr_in, lim_in, ind_in, h0_in, vk_in, hk_in, ik_in, hw_in,
     disp_out, hid_out,
     fl, fr, fp, edge, edge_l, edge_r, lim, ind, vk, ik, hw,
-    lp, rc, rp, el, er, ins, tw, lg,
+    l3, rt, rg, mean, ins, toep, tw, lg,
     hr, hl, hrt, lm, hf, rf, dd, lk3, x4, xr, w4, win, ikf,
     local_sem, feat_send, feat_recv, hid_send, hid_recv, look_send, look_recv,
 ):
@@ -134,20 +134,20 @@
     lane8 = iota((8, COLS), 1)
     spread = one_hot(iota((8, COLS), 0) == lax.rem(lane8, 8))
     taps = dot(vk[...], spread)
-    lane_disp = lane8 // 8
+    lane_r = lane8 // 8
     eye = one_hot(iota((128, 128), 0) == iota((128, 128), 1))
     for b in range(3):
         for e in range(3):
             tap = [taps[((a * 3 + b) * 3 + e) * 8 :][:8] for a in range(3)]
             rows = []
-            for at in range(16):
+            for q in range(BLOCK + 2):
                 block = jnp.zeros((8, COLS), F32)
                 for a in range(3):
-                    block = jnp.where(lane_disp == at - a, tap[a], block)
+                    block = jnp.where(lane_r == q - 2 + a, tap[a], block)
                 rows.append(block)
-            toeplitz = jnp.concatenate(rows, 0).astype(BF16)
-            slot = (b * 3 + e) * 128
-            tw[:, slot : slot + 128] = dot_nt(eye, toeplitz).astype(BF16)
+            at = (b * 3 + e) * WINDOW
+            toep[at : at + WINDOW, :] = jnp.concatenate(rows, 0).astype(BF16)
+    tw[...] = dot_nt(eye, toep[...]).astype(BF16)
 
     head_rows = jnp.broadcast_to(hw[...].astype(F32), (128, HID)).astype(BF16)
     head = dot_nt(eye, head_rows).astype(BF16)
@@ -175,92 +175,116 @@
     def flag(ok):
         return jnp.where(ok, 1.0, 0.0).astype(F32)
 
-    chan = iota((CH, 128), 0)
-    perm = one_hot(iota((CH, 128), 1) == lax.rem(chan, 8) * PER_GROUP + chan // 8)
-    perm_ch = one_hot(
-        iota((CH, CH), 1) == lax.rem(iota((CH, CH), 0), 8) * PER_GROUP + iota((CH, CH), 0) // 8
-    )
+    for delta in range(-1, COLS + 1):
+        apart = jnp.bitwise_and(lane8 - delta, COLS - 1)
+        at = 8 * (delta + 1)
+        mean[at : at + 8, :] = jnp.where(apart < DISPS, 1.0 / PER_GROUP, 0.0)
+    in_group = jnp.where(lane8 // PER_GROUP == iota((8, COLS), 0), 1.0, 0.0)
+    lane_ch = iota((CH, COLS), 1)
+    eye_ch = one_hot(iota((CH, 128), 0) == iota((CH, 128), 1))
+    apart_block = iota((128, COLS), 1) - iota((128, COLS), 0) // 8
 
     def prepare(b):
-        lp[b] = dot(perm_ch, fl[b])
-        rc[b] = dot(perm_ch, fr[b])
-        rp[b] = dot(perm_ch, fp[b]) * flag(left_ok)
-
         def column(ref, row):
             line = ref[b].astype(F32)[row : row + 1]
-            return dot_nt(perm, jnp.broadcast_to(line, (128, 128)).astype(BF16))
-
-        left_col, right_col, right_right = column(edge_l, 2), column(edge_r, 0), column(edge_r, 1)
-        left_sum = jnp.zeros((8, COLS), F32)
-        right_sum = jnp.zeros((8, COLS), F32)
-        for c in range(PER_GROUP):
-            s = slice(8 * c, 8 * c + 8)
-            left_sum += left_col[s] * rp[b, s]
-            right_sum += right_col[s] * jnp.where(lane8 == 0, right_right[s], rc[b, s])
-        el[b] = left_sum
-        er[b] = right_sum * flag(right_ok)
-
-    scale = [flag(row_ok[r]) * (1.0 / PER_GROUP) for r in (-1, 0, 1)]
-
-    def correlate(rows):
-        def pair(k, carry):
-            for b in rows:
-                found = ([], [], [])
-                for u in range(2):
-                    d = 2 * k - 1 + u
-                    turn = jnp.maximum(d, 0)
-                    factor = jnp.where((d >= 0) & (d < DISPS), scale[b], 0.0)
-                    keep = lane8 < COLS - turn
-                    total = jnp.zeros((8, COLS), F32)
-                    for c in range(PER_GROUP):
-                        s = slice(8 * c, 8 * c + 8)
-                        mixed = jnp.where(keep, rc[b, s], rp[b, s])
-                        total += pltpu.roll(mixed, turn, 1) * lp[b, s]
-                    raw = total * factor
-                    left = pltpu.roll(el[b], turn, 1) * factor
-                    right = pltpu.roll(er[b], turn, 1) * factor
-                    found[0].append(pltpu.roll(jnp.where(lane8 == COLS - 1, left, raw), 1, 1))
-                    found[1].append(raw)
-                    found[2].append(pltpu.roll(jnp.where(lane8 == 0, right, raw), COLS - 1, 1))
-                at = pl.multiple_of(16 * k, 16)
-                for e in range(3):
-                    ins[b, e, pl.ds(at, 16), :] = jnp.concatenate(found[e], 0).astype(BF16)
-            return carry
-
-        lax.fori_loop(0, PAIRS, pair, 0)
+            return dot_nt(eye_ch, jnp.broadcast_to(line, (128, 128)).astype(BF16))
+
+        there = flag(row_ok[b - 1])
+        own = fl[b].astype(F32) * there
+        before = column(edge_l, 2) * (there * flag(left_ok))
+        after = column(edge_r, 0) * (there * flag(right_ok))
+        l3[b, :, 0:128] = jnp.where(lane_ch == 0, before, pltpu.roll(own, 1, 1)).astype(BF16)
+        l3[b, :, 128:256] = own.astype(BF16)
+        l3[b, :, 256:384] = jnp.where(
+            lane_ch == COLS - 1, after, pltpu.roll(own, COLS - 1, 1)
+        ).astype(BF16)
+        rt[0, 0:COLS, :] = dot_nt(eye, jnp.concatenate([fr[b], pad], 0))
+        rt[0, COLS : COLS + 8, :] = edge_r[b].astype(F32)[0:8]
+        rt[1, 0:COLS, :] = dot_nt(eye, jnp.concatenate([fp[b], pad], 0)) * flag(left_ok)
+        for side in range(2):
+            for k in range(COLS // 2):
+                rows = [
+                    jnp.broadcast_to(rt[side, 2 * k + u : 2 * k + u + 1, :], (8, COLS)) * in_group
+                    for u in range(2)
+                ]
+                rg[side, 16 * k : 16 * k + 16, :] = jnp.concatenate(rows, 0).astype(BF16)
+        last = jnp.broadcast_to(rt[0, COLS + 1 : COLS + 2, :], (8, COLS)) * in_group
+        rg[0, 8 * COLS : 8 * COLS + 16, :] = jnp.concatenate([last, last], 0).astype(BF16)
+
+    def correlate(b):
+        left3 = l3[b]
+        beyond = dot(rg[0, 8 * COLS : 8 * COLS + 16, 0:CH], left3[:, 256:384])[0:8]
+        tail = [None] * 3
+        for blk in range(8):
+            rows = slice(128 * blk, 128 * blk + 128)
+            own3 = dot(rg[0, rows, 0:CH], left3)
+            near3 = dot(rg[1, rows, 0:CH], left3) if blk >= 2 else None
+            for e in range(3):
+                found = own3[:, 128 * e : 128 * e + 128]
+                first = BLOCK * blk - e + 1
+                if near3 is not None:
+                    found = jnp.where(
+                        apart_block >= first, found, near3[:, 128 * e : 128 * e + 128]
+                    )
+                if blk == 0 and e == 2:
+                    found = jnp.concatenate(
+                        [jnp.where(lane8 == COLS - 1, beyond, found[0:8]), found[8:]], 0
+                    )
+                at = 8 * (first + 1)
+                found = found * mean[at : at + 128, :]
+                if e == 0:
+                    ins[b, 0, 128 * blk + 16 : 128 * blk + 144, :] = found.astype(BF16)
+                    if blk == 7:
+                        ins[b, 0, 0:16, :] = found[112:128].astype(BF16)
+                elif e == 2:
+                    ins[b, 2, rows, :] = found.astype(BF16)
+                    if blk == 0:
+                        ins[b, 2, 1024:1040, :] = found[0:16].astype(BF16)
+                else:
+                    if blk == 0:
+                        head8 = found[0:8]
+                        ins[b, 1, 16:128, :] = found[8:120].astype(BF16)
+                    else:
+                        joined = jnp.concatenate([tail, found[0:120]], 0)
+                        ins[b, 1, rows, :] = joined.astype(BF16)
+                    tail = found[120:128]
+        ins[b, 1, 0:16, :] = jnp.concatenate([tail, head8], 0).astype(BF16)
+        ins[b, 1, 1024:1040, :] = jnp.concatenate([tail, head8], 0).astype(BF16)
 
     for key in [(0, -1, "p"), (0, -1, "e"), (0, 1, "e")]:
         feats[key].wait_recv()
     prepare(1)
-    correlate([1])
+    correlate(1)
     for key in feats:
         if key[0] != 0:
             feats[key].wait_recv()
-    prepare(0)
-    prepare(2)
-    correlate([0, 2])
+    for b in (0, 2):
+        prepare(b)
+        correlate(b)
 
     gain = jnp.zeros((8, COLS), F32)
     for g in range(GROUPS):
         gain = jnp.where(iota((8, COLS), 0) == g, gain_ref[g], gain)
-    at_disp = [jnp.broadcast_to(ind[t], (8, COLS)) for t in range(ITERS)]
+    at_rho = [
+        jnp.broadcast_to(jnp.bitwise_and(lane8[0:1] - ind[t], COLS - 1), (8, COLS))
+        for t in range(ITERS)
+    ]
     looked = [jnp.zeros((8, COLS), F32) for _ in range(ITERS)]
-    for j in range(7):
-        first = BLOCK * 8 * j
-        windows = [ins[b, e, first : first + 128, :] for b in range(3) for e in range(3)]
-        conv = dot(tw[0 : BLOCK * 8, :], jnp.concatenate(windows, 0))
-        raw = windows[4].astype(F32)[8 : 8 + BLOCK * 8]
+    for blk in range(8):
+        rows = slice(128 * blk, 128 * blk + WINDOW)
+        windows = [ins[b, e, rows, :] for b in range(3) for e in range(3)]
+        conv = dot(tw[...], jnp.concatenate(windows, 0))
+        raw = windows[4].astype(F32)[8:136]
         volume = (raw + jnp.maximum(conv, 0.0)).astype(BF16).astype(F32)
         volume = volume.reshape(BLOCK, 8, COLS)
-        count = min(BLOCK, DISPS - BLOCK * j)
-        lg[BLOCK * j : BLOCK * j + BLOCK, :] = jnp.sum(volume * gain[None], axis=1)
-        for q in range(count):
+        lg[BLOCK * blk : BLOCK * blk + BLOCK, :] = jnp.sum(volume * gain[None], axis=1)
+        for q in range(BLOCK):
             for t in range(ITERS):
-                looked[t] = jnp.where(at_disp[t] == BLOCK * j + q, volume[q], looked[t])
-
-    levels = iota((DISPS, COLS), 0)
+                looked[t] = jnp.where(at_rho[t] == BLOCK * blk + q, volume[q], looked[t])
+
+    levels = jnp.bitwise_and(iota((COLS, COLS), 1) - iota((COLS, COLS), 0), COLS - 1)
     valid = levels < lim[...]
-    masked = jnp.where(valid, lg[0:DISPS, :], -1e30)
+    masked = jnp.where(valid, lg[...], -1e30)
     weights = jnp.where(valid, jnp.exp(masked - jnp.max(masked, axis=0, keepdims=True)), 0.0)
     moment = jnp.sum(weights * levels.astype(F32), axis=0, keepdims=True)
     disparity = moment / jnp.sum(weights, axis=0, keepdims=True) / 8.0
@@ -383,14 +407,14 @@
             pltpu.VMEM((216, 8), BF16),
             pltpu.VMEM((3, 9, 3, 384), BF16),
             pltpu.VMEM((1, HID), BF16),
-            pltpu.VMEM((3, CH, COLS), F32),
-            pltpu.VMEM((3, CH, COLS), F32),
-            pltpu.VMEM((3, CH, COLS), F32),
-            pltpu.VMEM((3, 8, COLS), F32),
-            pltpu.VMEM((3, 8, COLS), F32),
-            pltpu.VMEM((3, 3, PAIRS * 16, COLS), BF16),
-            pltpu.VMEM((128, 9 * 128), BF16),
-            pltpu.VMEM((104, COLS), F32),
+            pltpu.VMEM((3, CH, 3 * COLS), BF16),
+            pltpu.VMEM((2, COLS + 8, COLS), F32),
+            pltpu.VMEM((2, 8 * COLS + 16, COLS), BF16),
+            pltpu.VMEM((8 * (COLS + 2), COLS), F32),
+            pltpu.VMEM((3, 3, 8 * (COLS + 2), COLS), BF16),
+            pltpu.VMEM((9 * WINDOW, COLS), BF16),
+            pltpu.VMEM((128, 9 * WINDOW), BF16),
+            pltpu.VMEM((COLS, COLS), F32),
             pltpu.VMEM((ITERS, 5, COLS, HID), BF16),
             pltpu.VMEM((ITERS, 5, 16, HID), BF16),
             pltpu.VMEM((ITERS, 5, 16, HID), BF16),

time: 63.9 us -> 51.9 us (0.81)
  Pallas kernels: 60.5 us -> 48.6 us
    pallas_call x1, Pallas kernels: 60.5 us -> 48.6 us  [local(): pl.pallas_call(kernel, out_shape=(jax.ShapeDtypeStruct((1, COLS), F32), j...]
where the time goes in v1:
time: 51.9 us; the launch traced here: 51.7 us
  Pallas kernels  48.6 us (94%)
  local copies, waits for them, and re-layouts  2.51 us (5%)
  between operations  0.65 us (1%)
    pallas_call x1, Pallas kernels, local(): pl.pallas_call(kernel, out_shape=(jax.ShapeDtypeStruct((1, COLS), F32), j...  48.6 us
    unnamed x4, local copies, waits for them, and re-layouts  2.51 us

profile of v1, /device:TPU:1, one launch (start us, length us, event | category | flops | bytes accessed | tf_op | source)
XLA Modules:
  0.0 51.7 jit_solution(8847766767985914476)
XLA Ops:
  0.6 48.6 %stereo.1 = (f32[1,128]{1,0:T(1,128)}, bf16[128,128]{1,0:T(8,128)(2,1)}) custom-call(f32[8]{0:T(128)} %gain_ref.1, bf16[96,128]{1,0:T(8,128)(2,1)} %bitcast.13, bf16[96,128]{1,0:T(8,128)(2,1)} %bitcast.14, s32[1,128]{1,0:T(1,128)} %lim_in.1, s32[3,1,128]{2,1,0:T(1,128)} %ind_in.1, bf16[128,128]{1,0:T(8,128)(2,1)} %bitcast.11, bf16[216,8]{1,0:T(8,128)(2,1)} %bitcast.10, ...), custom_call_target="tpu_custom_call" | custom-call | tf_op jit(solution)/shard_map/stereo/pallas_call | solution.py:390
  49.2 0.0 copy-start
  49.2 0.6 %copy-done = f32[1,128]{1,0:T(1,128)S(1)} copy-done((f32[1,128]{1,0:T(1,128)S(1)}, f32[1,128]{1,0:T(1,128)}, u32[]{:S(2)}) %copy-start) | copy-done | bytes 536
  49.8 0.5 copy.14
  50.3 1.4 %copy.15 = bf16[1,128,128]{2,1,0:T(8,128)(2,1)} copy(bf16[1,128,128]{2,1,0:T(8,128)(2,1)} %bitcast.12) | data formatting | bytes 65536
Async XLA Ops:
  49.2 0.6 %copy-start = (f32[1,128]{1,0:T(1,128)S(1)}, f32[1,128]{1,0:T(1,128)}, u32[]{:S(2)}) copy-start(f32[1,128]{1,0:T(1,128)} %get-tuple-element.8) | copy-start | bytes 1540

commit v2 on v1

--- a/solution.py
+++ b/solution.py
@@ -17,10 +17,13 @@
 F32 = jnp.float32
 BF16 = jnp.bfloat16
 
-AROUND = [(r, c) for r in range(-2, 3) for c in (-1, 0, 1) if (r, c) != (0, 0)]
+REACH = 6
+ROWS = 2 * REACH + 1
+NEAR = [r for r in range(-REACH, REACH + 1) if r != 0]
 BLOCK = 16
 WINDOW = 8 * (BLOCK + 2)
 EXT = COLS + 16
+LOOK_AT = (0, 16, 24)
 NT = (((1,), (1,)), ((), ()))
 
 
@@ -45,7 +48,7 @@
     disp_out, hid_out,
     fl, fr, fp, edge, edge_l, edge_r, lim, ind, vk, ik, hw,
     l3, rt, rg, mean, ins, toep, tw, lg,
-    hr, hl, hrt, lm, hf, rf, dd, lk3, x4, xr, w4, win, ikf,
+    hr, hl, hrt, lm, hf, rf, dd, lk3, x4, up, part, w4, win, ikf,
     local_sem, feat_send, feat_recv, hid_send, hid_recv, look_send, look_recv,
 ):
     band, disp = lax.axis_index("band"), lax.axis_index("disp")
@@ -65,8 +68,10 @@
                 (hw_in, hw),
                 (lim_in, lim),
                 (ind_in, ind),
-                (h0_in, hr.at[0, 2]),
-                (hk_in, w4.at[:, 0:384, :]),
+                (h0_in, hr.at[REACH]),
+                (hk_in.at[0], w4.at[0:384, :]),
+                (hk_in.at[1], w4.at[512:896, :]),
+                (hk_in.at[2], w4.at[1024:1408, :]),
             ]
         )
     ]
@@ -74,8 +79,19 @@
         copy.start()
 
     barrier = pltpu.get_barrier_semaphore()
-    for r, c in AROUND:
-        pl.semaphore_signal(barrier, inc=1, device_id=device(r, c), device_id_type=MESH)
+    row_ok = {r: (band + r >= 0) & (band + r < bands) for r in range(-REACH, REACH + 1)}
+    left_ok, right_ok = disp > 0, disp < disps - 1
+    expected = jnp.int32(2)
+    for c in (-1, 1):
+        pl.semaphore_signal(barrier, inc=1, device_id=device(0, c), device_id_type=MESH)
+    for r in NEAR:
+        expected += jnp.where(row_ok[r], 3, 0)
+
+        @pl.when(row_ok[r])
+        def _(r=r):
+            for c in (-1, 0, 1):
+                pl.semaphore_signal(barrier, inc=1, device_id=device(r, c), device_id_type=MESH)
+
 
     locals_[0].wait()
     locals_[1].wait()
@@ -88,7 +104,7 @@
         + dot_nt(pick_right, jnp.concatenate([fr[1], pad], 0))
     ).astype(BF16)
 
-    pl.semaphore_wait(barrier, len(AROUND))
+    pl.semaphore_wait(barrier, expected)
 
     def remote(src, dst, send, recv, i, r, c):
         return pltpu.make_async_remote_copy(
@@ -96,38 +112,87 @@
             device_id=device(r, c), device_id_type=MESH,
         )
 
-    feats = {}
-    plan = [(r, -1, "p") for r in (0, -1, 1)] + [(r, -1, "e") for r in (0, -1, 1)]
-    plan += [(r, 1, "e") for r in (0, -1, 1)]
-    plan += [(r, 0, kind) for r in (-1, 1) for kind in ("l", "r")]
-    for i, (r, c, kind) in enumerate(plan):
-        src, dst = {
-            "p": (fr_in, fp.at[r + 1]),
-            "e": (edge, (edge_l if c < 0 else edge_r).at[r + 1]),
-            "l": (fl_in, fl.at[r + 1]),
-            "r": (fr_in, fr.at[r + 1]),
-        }[kind]
-        feats[(r, c, kind)] = remote(src, dst, feat_send, feat_recv, i, -r, -c)
-        feats[(r, c, kind)].start()
-
-    def hidden_copies(t):
-        copies = []
-        for i, (r, c) in enumerate(AROUND):
-            own = h0_in if t == 0 else hr.at[t, 2]
-            if c == 0:
-                src, dst = own, hr.at[t, r + 2]
-            elif c < 0:
-                src, dst = own.at[COLS - 16 : COLS], hl.at[t, r + 2]
-            else:
-                src, dst = own.at[0:16], hrt.at[t, r + 2]
-            copies.append(
-                remote(src, dst, hid_send.at[t], hid_recv.at[t], i, -r, -c)
+    def grouped(make):
+        groups = {r: [] for r in range(-REACH, REACH + 1)}
+        for r, c, copy in make:
+            groups[r].append((c, copy))
+        return groups
+
+    def start(groups, r):
+        if r == 0:
+            for _, copy in groups[r]:
+                copy.start()
+        else:
+
+            @pl.when(row_ok[-r])
+            def _():
+                for _, copy in groups[r]:
+                    copy.start()
+
+    def arrive(groups, r):
+        if r == 0:
+            for _, copy in groups[r]:
+                copy.wait_recv()
+        else:
+
+            @pl.when(row_ok[r])
+            def _():
+                for _, copy in groups[r]:
+                    copy.wait_recv()
+
+    def leave(groups, r):
+        if r == 0:
+            for _, copy in groups[r]:
+                copy.wait_send()
+        else:
+
+            @pl.when(row_ok[-r])
+            def _():
+                for _, copy in groups[r]:
+                    copy.wait_send()
+
+    feat_make = []
+    for r in (0, -1, 1):
+        kinds = [(-1, fr_in, fp.at[r + 1]), (-1, edge, edge_l.at[r + 1]), (1, edge, edge_r.at[r + 1])]
+        if r != 0:
+            kinds += [(0, fl_in, fl.at[r + 1]), (0, fr_in, fr.at[r + 1])]
+        for c, src, dst in kinds:
+            i = len(feat_make)
+            feat_make.append((r, c, remote(src, dst, feat_send, feat_recv, i, -r, -c)))
+    feats = grouped(feat_make)
+    for r in (0, -1, 1):
+        start(feats, r)
+
+    hid_make, look_make = [], []
+    for r in range(-REACH, REACH + 1):
+        for c in (-1, 0, 1):
+            if (r, c) == (0, 0):
+                continue
+            i, at = len(hid_make), r + REACH
+            src, dst = {
+                0: (h0_in, hr.at[at]),
+                -1: (h0_in.at[COLS - 8 : COLS], hl.at[at]),
+                1: (h0_in.at[0:8], hrt.at[at]),
+            }[c]
+            hid_make.append((r, c, remote(src, dst, hid_send, hid_recv, i, -r, -c)))
+            deep = 32 if abs(r) <= 4 else 16
+            look_make.append(
+                (
+                    r,
+                    c,
+                    remote(
+                        lm.at[REACH, 1, 0:deep],
+                        lm.at[at, c + 1, 0:deep],
+                        look_send,
+                        look_recv,
+                        i,
+                        -r,
+                        -c,
+                    ),
+                )
             )
-        return copies
-
-    hidden_sent = [hidden_copies(0)]
-    for copy in hidden_sent[0]:
-        copy.start()
+    hids, looks = grouped(hid_make), grouped(look_make)
+    order = [0] + [r * side for r in range(1, REACH + 1) for side in (-1, 1)]
 
     for copy in locals_[2:]:
         copy.wait()
@@ -160,7 +225,7 @@
     source = iota((128, 32), 1)
     source_i, source_b = source // 3, lax.rem(source, 3)
     for t in range(ITERS):
-        goes_to = 32 * source_b + jnp.where(source_i < GROUPS, 8 * t + source_i, 24)
+        goes_to = 32 * source_b + jnp.where(source_i < GROUPS, LOOK_AT[t] + source_i, 8)
         move = one_hot((source < 27) & (iota((128, 32), 0) == goes_to))
         for a in range(3):
             win[t, a] = dot(move, ikf[a].astype(BF16)).astype(BF16)
@@ -168,9 +233,6 @@
     hf[...] = jnp.zeros_like(hf)
     rf[...] = jnp.zeros_like(rf)
     dd[...] = jnp.zeros_like(dd)
-
-    row_ok = {r: (band + r >= 0) & (band + r < bands) for r in range(-2, 3)}
-    left_ok, right_ok = disp > 0, disp < disps - 1
 
     def flag(ok):
         return jnp.where(ok, 1.0, 0.0).astype(F32)
@@ -251,13 +313,13 @@
         ins[b, 1, 0:16, :] = jnp.concatenate([tail, head8], 0).astype(BF16)
         ins[b, 1, 1024:1040, :] = jnp.concatenate([tail, head8], 0).astype(BF16)
 
-    for key in [(0, -1, "p"), (0, -1, "e"), (0, 1, "e")]:
-        feats[key].wait_recv()
+    arrive(feats, 0)
     prepare(1)
     correlate(1)
-    for key in feats:
-        if key[0] != 0:
-            feats[key].wait_recv()
+    for r in (-1, 1):
+        arrive(feats, r)
+    for r in order:
+        start(hids, r)
     for b in (0, 2):
         prepare(b)
         correlate(b)
@@ -294,90 +356,130 @@
     low = disparity - high - middle
     sub8 = iota((8, COLS), 0)
     parts = jnp.zeros((8, COLS), F32)
-    for i, part in enumerate((high, middle, low)):
-        parts = jnp.where(sub8 == i, part, parts)
-    lm[2, 1] = jnp.concatenate(looked + [parts], 0).astype(BF16)
-    look_copies = [
-        remote(lm.at[2, 1], lm.at[r + 2, c + 1], look_send, look_recv, i, -r, -c)
-        for i, (r, c) in enumerate(AROUND)
-    ]
-    for copy in look_copies:
-        copy.start()
-    for copy in look_copies:
-        copy.wait_recv()
+    for i, piece in enumerate((high, middle, low)):
+        parts = jnp.where(sub8 == i, piece, parts)
+    lm[REACH, 1] = jnp.concatenate([looked[0], parts, looked[1], looked[2]], 0).astype(BF16)
+    for r in order:
+        start(looks, r)
+
+    def side_by_side(ref, i):
+        for b in range(3):
+            x4[i, :, 128 * b : 128 * b + 128] = ref[i, 7 + b : 7 + b + EXT, :].astype(BF16)
+
+    def taps_of(low, high, lanes):
+        return jnp.concatenate(
+            [
+                x4[low - 1 + a : high - 1 + a, :, lanes].reshape((high - low) * EXT, -1)
+                for a in range(3)
+            ],
+            1,
+        )
+
+    def chunks(low, high):
+        half = (high - low + 1) // 2 if high - low > 5 else high - low
+        return [(k, min(k + half, high)) for k in range(low, high, half)]
+
+    for r in order:
+        arrive(hids, r)
+    for r in range(-REACH, REACH + 1):
+        i = r + REACH
+        hf[i, 16 : 16 + COLS, :] = jnp.where(row_ok[r], hr[i].astype(F32), 0.0)
+        hf[i, 8:16, :] = jnp.where(row_ok[r] & left_ok, hl[i].astype(F32), 0.0)
+        hf[i, 16 + COLS : 24 + COLS, :] = jnp.where(
+            row_ok[r] & right_ok, hrt[i].astype(F32), 0.0
+        )
+        side_by_side(hf, i)
+    hid_taps = jnp.concatenate([w4[512 * a : 512 * a + 384, 0:256] for a in range(3)], 0)
+    for low, high in chunks(1, ROWS - 1):
+        part[low:high] = dot(taps_of(low, high, slice(0, 384)), hid_taps).reshape(
+            high - low, EXT, 256
+        )
+    lane_ext = iota((EXT, 128), 1)
+    col = iota((EXT, 128), 0)
+    inside = jnp.where(
+        (col < 8) & jnp.logical_not(left_ok) | (col >= 8 + COLS) & jnp.logical_not(right_ok), 0.0, 1.0
+    )
+
+    for r in order:
+        arrive(looks, r)
 
     lane32 = iota((32, COLS), 1)
     place = one_hot(iota((EXT, 256), 0) == iota((EXT, 256), 1))
-    take = one_hot((iota((128, 128), 0) >= 56) & (iota((128, 128), 0) < 59))
-    for r in range(-2, 3):
+    take = one_hot((iota((128, 128), 0) >= 40) & (iota((128, 128), 0) < 43))
+    zero = jnp.zeros((32, COLS), F32)
+    for r in range(-REACH, REACH + 1):
+        i = r + REACH
+
         def tile(c, ok):
-            return jnp.where(ok, lm[r + 2, c + 1].astype(F32), 0.0)
+            if abs(r) <= 4:
+                return jnp.where(ok, lm[i, c + 1].astype(F32), 0.0)
+            return jnp.concatenate(
+                [jnp.where(ok, lm[i, c + 1, 0:16].astype(F32), 0.0), zero[0:16]], 0
+            )
 
         left, own, right = (
             tile(-1, row_ok[r] & left_ok), tile(0, row_ok[r]), tile(1, row_ok[r] & right_ok)
         )
         lows, highs = [], []
-        for s in (-1, 0, 1):
-            lows.append(pltpu.roll(jnp.where(lane32 < 120 + s, own, left), 8 - s, 1))
-            highs.append(pltpu.roll(jnp.where(lane32 < 120 + s, right, own), 8 - s, 1))
-        zero = jnp.zeros((32, COLS), F32)
+        for shift in (-1, 0, 1):
+            lows.append(pltpu.roll(jnp.where(lane32 < 120 + shift, own, left), 8 - shift, 1))
+            highs.append(pltpu.roll(jnp.where(lane32 < 120 + shift, right, own), 8 - shift, 1))
         wide = jnp.concatenate(
             [jnp.concatenate(lows + [zero], 0), jnp.concatenate(highs + [zero], 0)], 1
         ).astype(BF16)
         found = dot_nt(place, wide)
-        lk3[r + 2] = found
-        dd[r + 2, 8 : 8 + EXT, :] = dot(found.astype(BF16), take)
-
-    lane_ext = iota((EXT, 128), 1)
+        lk3[i] = found
+        dd[i, 8 : 8 + EXT, :] = dot(found.astype(BF16), take)
+
     for t in range(ITERS):
-        for copy in hidden_sent[t]:
-            copy.wait_recv()
-        for r in range(-2, 3):
-            i = r + 2
-            own = jnp.where(row_ok[r], hr[t, i].astype(F32), 0.0)
-            left = jnp.where(row_ok[r] & left_ok, hl[t, i].astype(F32), 0.0)
-            right = jnp.where(row_ok[r] & right_ok, hrt[t, i].astype(F32), 0.0)
-            hf[i, 16 : 16 + COLS, :] = own
-            hf[i, 8:16, :] = left[8:16]
-            hf[i, 16 + COLS : 24 + COLS, :] = right[0:8]
-            for b in range(3):
-                x4[i, :, 128 * b : 128 * b + 128] = hf[i, 7 + b : 7 + b + EXT, :].astype(BF16)
+        reach = REACH - 2 * t
+        low, high = REACH - reach, REACH + reach + 1
+        for a in range(3):
+            w4[512 * a + 384 : 512 * a + 512, :] = win[t, a]
+        for i in range(low, high):
             if t > 0:
+                side_by_side(hf, i)
                 dd[i, 8 : 8 + EXT, :] += dot(x4[i, :, 128:256], head)
             inputs = lk3[i]
             for b in range(3):
                 shifted = 0.25 * dd[i, 7 + b : 7 + b + EXT, :]
-                inputs = jnp.where(lane_ext == 32 * b + 24, shifted, inputs)
+                inputs = jnp.where(lane_ext == 32 * b + 8, shifted, inputs)
             x4[i, :, 384:512] = inputs.astype(BF16)
-        for a in range(3):
-            w4[a, 384:512, :] = win[t, a]
-        gates = jnp.zeros((3 * EXT, 256), F32)
-        for a in range(3):
-            gates += dot(x4[a : a + 3].reshape(3 * EXT, 512), w4[a, :, 0:256])
-        update = jax.nn.sigmoid(gates[EXT : 2 * EXT, 0:128])
-        reset = jax.nn.sigmoid(gates[:, 128:256]).reshape(3, EXT, 128)
-        rf[:, 8 : 8 + EXT, :] = reset * hf[1:4, 8 : 8 + EXT, :]
-        pre = jnp.zeros((EXT, 128), F32)
-        for a in range(3):
-            for b in range(3):
-                xr[:, 128 * b : 128 * b + 128] = rf[a, 7 + b : 7 + b + EXT, :].astype(BF16)
-            xr[:, 384:512] = x4[a + 1, :, 384:512]
-            pre += dot(xr[...], w4[a, :, 256:384])
-        candidate = jnp.tanh(pre)
-        fresh = (1.0 - update) * hf[2, 8 : 8 + EXT, :] + update * candidate
-        fresh = fresh[8 : 8 + COLS].astype(BF16)
-        disparity += dot_nt(head_row, fresh)[0:1]
-        if t < ITERS - 1:
-            hr[t + 1, 2] = fresh
-            hidden_sent.append(hidden_copies(t + 1))
-            for copy in hidden_sent[t + 1]:
-                copy.start()
-        else:
-            hid_out[...] = fresh
+        for first, last in chunks(low + 1, high - 1):
+            count = last - first
+            if t == 0:
+                in_taps = jnp.concatenate([win[0, a, :, 0:256] for a in range(3)], 0)
+                gates = dot(taps_of(first, last, slice(384, 512)), in_taps)
+                gates = gates.reshape(count, EXT, 256) + part[first:last]
+            else:
+                gates = dot(taps_of(first, last, slice(0, 512)), w4[:, 0:256])
+                gates = gates.reshape(count, EXT, 256)
+            up[first:last] = jax.nn.sigmoid(gates[:, :, 0:128])
+            reset = jax.nn.sigmoid(gates[:, :, 128:256])
+            rf[first:last, 8 : 8 + EXT, :] = reset * hf[first:last, 8 : 8 + EXT, :]
+        for i in range(low + 1, high - 1):
+            side_by_side(rf, i)
+        for first, last in chunks(low + 2, high - 2):
+            count = last - first
+            pre = dot(taps_of(first, last, slice(0, 512)), w4[:, 256:384])
+            candidate = jnp.tanh(pre).reshape(count, EXT, 128)
+            update = up[first:last]
+            fresh = (1.0 - update) * hf[first:last, 8 : 8 + EXT, :] + update * candidate
+            if t < ITERS - 1:
+                for i in range(first, last):
+                    kept = fresh[i - first] * (inside * flag(row_ok[i - REACH]))
+                    hf[i, 8 : 8 + EXT, :] = kept.astype(BF16).astype(F32)
+            else:
+                hf[REACH, 8 : 8 + EXT, :] = fresh[0].astype(BF16).astype(F32)
+        own = hf[REACH, 16 : 16 + COLS, :].astype(BF16)
+        disparity += dot_nt(head_row, own)[0:1]
+    hid_out[...] = own
     disp_out[...] = disparity
 
-    for copy in list(feats.values()) + look_copies + sum(hidden_sent, []):
-        copy.wait_send()
+    for groups in (feats, hids, looks):
+        for r in groups:
+            if groups[r]:
+                leave(groups, r)
 
 
 def local(
@@ -415,26 +517,27 @@
             pltpu.VMEM((9 * WINDOW, COLS), BF16),
             pltpu.VMEM((128, 9 * WINDOW), BF16),
             pltpu.VMEM((COLS, COLS), F32),
-            pltpu.VMEM((ITERS, 5, COLS, HID), BF16),
-            pltpu.VMEM((ITERS, 5, 16, HID), BF16),
-            pltpu.VMEM((ITERS, 5, 16, HID), BF16),
-            pltpu.VMEM((5, 3, 32, COLS), BF16),
-            pltpu.VMEM((5, EXT + 16, 128), F32),
-            pltpu.VMEM((3, EXT + 16, 128), F32),
-            pltpu.VMEM((5, EXT + 16, 128), F32),
-            pltpu.VMEM((5, EXT, 128), F32),
-            pltpu.VMEM((5, EXT, 512), BF16),
-            pltpu.VMEM((EXT, 512), BF16),
-            pltpu.VMEM((3, 512, 384), BF16),
+            pltpu.VMEM((ROWS, COLS, HID), BF16),
+            pltpu.VMEM((ROWS, 8, HID), BF16),
+            pltpu.VMEM((ROWS, 8, HID), BF16),
+            pltpu.VMEM((ROWS, 3, 32, COLS), BF16),
+            pltpu.VMEM((ROWS, EXT + 16, 128), F32),
+            pltpu.VMEM((ROWS, EXT + 16, 128), F32),
+            pltpu.VMEM((ROWS, EXT + 16, 128), F32),
+            pltpu.VMEM((ROWS, EXT, 128), F32),
+            pltpu.VMEM((ROWS, EXT, 512), BF16),
+            pltpu.VMEM((ROWS, EXT, 128), F32),
+            pltpu.VMEM((ROWS, EXT, 256), F32),
+            pltpu.VMEM((3 * 512, 384), BF16),
             pltpu.VMEM((ITERS, 3, 128, 384), BF16),
             pltpu.VMEM((3, 32, 384), F32),
-            dma((9,)),
+            dma((11,)),
             dma((13,)),
             dma((13,)),
-            dma((ITERS, len(AROUND))),
-            dma((ITERS, len(AROUND))),
-            dma((len(AROUND),)),
-            dma((len(AROUND),)),
+            dma((3 * ROWS - 1,)),
+            dma((3 * ROWS - 1,)),
+            dma((3 * ROWS - 1,)),
+            dma((3 * ROWS - 1,)),
         ],
         compiler_params=pltpu.CompilerParams(collective_id=0, has_side_effects=True),
         name="stereo",

time: 51.9 us -> 41.8 us (0.81)
  the two profiles are of different devices: /device:TPU:1 before, /device:TPU:68 now
where the time goes in v2:
time: 41.8 us; the launch traced here: 41.5 us
  Pallas kernels  38.4 us (92%)
  local copies, waits for them, and re-layouts  2.51 us (6%)
  between operations  0.65 us (2%)
    pallas_call x1, Pallas kernels, local(): pl.pallas_call(kernel, out_shape=(jax.ShapeDtypeStruct((1, COLS), F32), j...  38.4 us
    unnamed x4, local copies, waits for them, and re-layouts  2.51 us

profile of v2, /device:TPU:68, one launch (start us, length us, event | category | flops | bytes accessed | tf_op | source)
XLA Modules:
  0.0 41.5 jit_solution(18092465287698325552)
XLA Ops:
  0.6 38.4 %stereo.1 = (f32[1,128]{1,0:T(1,128)}, bf16[128,128]{1,0:T(8,128)(2,1)}) custom-call(f32[8]{0:T(128)} %gain_ref.1, bf16[96,128]{1,0:T(8,128)(2,1)} %bitcast.13, bf16[96,128]{1,0:T(8,128)(2,1)} %bitcast.14, s32[1,128]{1,0:T(1,128)} %lim_in.1, s32[3,1,128]{2,1,0:T(1,128)} %ind_in.1, bf16[128,128]{1,0:T(8,128)(2,1)} %bitcast.11, bf16[216,8]{1,0:T(8,128)(2,1)} %bitcast.10, ...), custom_call_target="tpu_custom_call" | custom-call | tf_op jit(solution)/shard_map/stereo/pallas_call | solution.py:492
  39.0 0.0 copy-start
  39.0 0.6 %copy-done = f32[1,128]{1,0:T(1,128)S(1)} copy-done((f32[1,128]{1,0:T(1,128)S(1)}, f32[1,128]{1,0:T(1,128)}, u32[]{:S(2)}) %copy-start) | copy-done | bytes 536
  39.7 0.5 %copy.14 = f32[1,128]{1,0:T(1,128)} copy(f32[1,128]{1,0:T(1,128)S(1)} %copy-done) | data formatting | bytes 1024
  40.2 1.4 %copy.15 = bf16[1,128,128]{2,1,0:T(8,128)(2,1)} copy(bf16[1,128,128]{2,1,0:T(8,128)(2,1)} %bitcast.12) | data formatting | bytes 65536
Async XLA Ops:
  39.0 0.6 %copy-start = (f32[1,128]{1,0:T(1,128)S(1)}, f32[1,128]{1,0:T(1,128)}, u32[]{:S(2)}) copy-start(f32[1,128]{1,0:T(1,128)} %get-tuple-element.8) | copy-start | bytes 1540

commit v3 on v2

--- a/solution.py
+++ b/solution.py
@@ -49,7 +49,7 @@
     fl, fr, fp, edge, edge_l, edge_r, lim, ind, vk, ik, hw,
     l3, rt, rg, mean, ins, toep, tw, lg,
     hr, hl, hrt, lm, hf, rf, dd, lk3, x4, up, part, w4, win, ikf,
-    local_sem, feat_send, feat_recv, hid_send, hid_recv, look_send, look_recv,
+    local_sem, feat_send, feat_recv, hid_send, hid_recv, look_send, look_recv, known,
 ):
     band, disp = lax.axis_index("band"), lax.axis_index("disp")
     bands, disps = lax.axis_size("band"), lax.axis_size("disp")
@@ -81,17 +81,30 @@
     barrier = pltpu.get_barrier_semaphore()
     row_ok = {r: (band + r >= 0) & (band + r < bands) for r in range(-REACH, REACH + 1)}
     left_ok, right_ok = disp > 0, disp < disps - 1
-    expected = jnp.int32(2)
-    for c in (-1, 1):
-        pl.semaphore_signal(barrier, inc=1, device_id=device(0, c), device_id_type=MESH)
-    for r in NEAR:
-        expected += jnp.where(row_ok[r], 3, 0)
-
-        @pl.when(row_ok[r])
-        def _(r=r):
-            for c in (-1, 0, 1):
-                pl.semaphore_signal(barrier, inc=1, device_id=device(r, c), device_id_type=MESH)
-
+    col_ok = {-1: left_ok, 0: None, 1: right_ok}
+
+    def there(r, c):
+        if r == 0:
+            return col_ok[c]
+        return row_ok[r] if c == 0 else row_ok[r] & col_ok[c]
+
+    def when(condition, action):
+        if condition is None:
+            action()
+        else:
+            pl.when(condition)(action)
+
+    def count(conditions):
+        return sum(jnp.where(ok, 1, 0).astype(jnp.int32) for ok in conditions)
+
+    nearest = [(r, c) for r in (-1, 0, 1) for c in (-1, 0, 1) if (r, c) != (0, 0)]
+    for r, c in nearest:
+        when(
+            there(r, c),
+            lambda r=r, c=c: pl.semaphore_signal(
+                barrier, inc=1, device_id=device(r, c), device_id_type=MESH
+            ),
+        )
 
     locals_[0].wait()
     locals_[1].wait()
@@ -104,7 +117,21 @@
         + dot_nt(pick_right, jnp.concatenate([fr[1], pad], 0))
     ).astype(BF16)
 
-    pl.semaphore_wait(barrier, expected)
+    pl.semaphore_wait(barrier, count(there(r, c) for r, c in nearest))
+
+    def tell(step, r):
+        for way in (-r, r):
+            when(
+                there(way, 0),
+                lambda way=way: pl.semaphore_signal(
+                    known.at[step], inc=1, device_id=device(way, 0), device_id_type=MESH
+                ),
+            )
+
+    def learn(step, r):
+        pl.semaphore_wait(known.at[step], count((there(-r, 0), there(r, 0))))
+
+    tell(0, 1)
 
     def remote(src, dst, send, recv, i, r, c):
         return pltpu.make_async_remote_copy(
@@ -118,38 +145,22 @@
             groups[r].append((c, copy))
         return groups
 
+    def each(groups, r, ok_of, action):
+        def row():
+            for c, copy in groups[r]:
+                when(None if c == 0 else ok_of(0, c), lambda copy=copy: action(copy))
+
+        if groups[r]:
+            when(ok_of(r, 0), row)
+
     def start(groups, r):
-        if r == 0:
-            for _, copy in groups[r]:
-                copy.start()
-        else:
-
-            @pl.when(row_ok[-r])
-            def _():
-                for _, copy in groups[r]:
-                    copy.start()
+        each(groups, r, lambda r, c: there(-r, -c), lambda copy: copy.start())
 
     def arrive(groups, r):
-        if r == 0:
-            for _, copy in groups[r]:
-                copy.wait_recv()
-        else:
-
-            @pl.when(row_ok[r])
-            def _():
-                for _, copy in groups[r]:
-                    copy.wait_recv()
+        each(groups, r, there, lambda copy: copy.wait_recv())
 
     def leave(groups, r):
-        if r == 0:
-            for _, copy in groups[r]:
-                copy.wait_send()
-        else:
-
-            @pl.when(row_ok[-r])
-            def _():
-                for _, copy in groups[r]:
-                    copy.wait_send()
+        each(groups, r, lambda r, c: there(-r, -c), lambda copy: copy.wait_send())
 
     feat_make = []
     for r in (0, -1, 1):
@@ -251,18 +262,21 @@
             line = ref[b].astype(F32)[row : row + 1]
             return dot_nt(eye_ch, jnp.broadcast_to(line, (128, 128)).astype(BF16))
 
-        there = flag(row_ok[b - 1])
-        own = fl[b].astype(F32) * there
-        before = column(edge_l, 2) * (there * flag(left_ok))
-        after = column(edge_r, 0) * (there * flag(right_ok))
+        def kept(ok, value):
+            return jnp.where(ok, value.astype(F32), 0.0)
+
+        row, row_left, row_right = (row_ok[b - 1], row_ok[b - 1] & left_ok, row_ok[b - 1] & right_ok)
+        own = kept(row, fl[b])
+        before = kept(row_left, column(edge_l, 2))
+        after = kept(row_right, column(edge_r, 0))
         l3[b, :, 0:128] = jnp.where(lane_ch == 0, before, pltpu.roll(own, 1, 1)).astype(BF16)
         l3[b, :, 128:256] = own.astype(BF16)
         l3[b, :, 256:384] = jnp.where(
             lane_ch == COLS - 1, after, pltpu.roll(own, COLS - 1, 1)
         ).astype(BF16)
-        rt[0, 0:COLS, :] = dot_nt(eye, jnp.concatenate([fr[b], pad], 0))
-        rt[0, COLS : COLS + 8, :] = edge_r[b].astype(F32)[0:8]
-        rt[1, 0:COLS, :] = dot_nt(eye, jnp.concatenate([fp[b], pad], 0)) * flag(left_ok)
+        rt[0, 0:COLS, :] = dot_nt(eye, jnp.concatenate([kept(row, fr[b]).astype(BF16), pad], 0))
+        rt[0, COLS : COLS + 8, :] = kept(row_right, edge_r[b])[0:8]
+        rt[1, 0:COLS, :] = dot_nt(eye, jnp.concatenate([kept(row_left, fp[b]).astype(BF16), pad], 0))
         for side in range(2):
             for k in range(COLS // 2):
                 rows = [
@@ -313,16 +327,26 @@
         ins[b, 1, 0:16, :] = jnp.concatenate([tail, head8], 0).astype(BF16)
         ins[b, 1, 1024:1040, :] = jnp.concatenate([tail, head8], 0).astype(BF16)
 
+    learn(0, 1)
+    tell(1, 2)
     arrive(feats, 0)
     prepare(1)
     correlate(1)
     for r in (-1, 1):
         arrive(feats, r)
-    for r in order:
+    for r in order[:5]:
         start(hids, r)
-    for b in (0, 2):
-        prepare(b)
-        correlate(b)
+    learn(1, 2)
+    tell(2, 2)
+    for r in order[5:9]:
+        start(hids, r)
+    prepare(0)
+    correlate(0)
+    learn(2, 2)
+    for r in order[9:]:
+        start(hids, r)
+    prepare(2)
+    correlate(2)
 
     gain = jnp.zeros((8, COLS), F32)
     for g in range(GROUPS):
@@ -400,14 +424,20 @@
         (col < 8) & jnp.logical_not(left_ok) | (col >= 8 + COLS) & jnp.logical_not(right_ok), 0.0, 1.0
     )
 
-    for r in order:
-        arrive(looks, r)
-
     lane32 = iota((32, COLS), 1)
     place = one_hot(iota((EXT, 256), 0) == iota((EXT, 256), 1))
     take = one_hot((iota((128, 128), 0) >= 40) & (iota((128, 128), 0) < 43))
     zero = jnp.zeros((32, COLS), F32)
-    for r in range(-REACH, REACH + 1):
+
+    def inputs_of(i):
+        inputs = lk3[i]
+        for b in range(3):
+            shifted = 0.25 * dd[i, 7 + b : 7 + b + EXT, :]
+            inputs = jnp.where(lane_ext == 32 * b + 8, shifted, inputs)
+        x4[i, :, 384:512] = inputs.astype(BF16)
+
+    for r in order:
+        arrive(looks, r)
         i = r + REACH
 
         def tile(c, ok):
@@ -430,39 +460,35 @@
         found = dot_nt(place, wide)
         lk3[i] = found
         dd[i, 8 : 8 + EXT, :] = dot(found.astype(BF16), take)
+        inputs_of(i)
 
     for t in range(ITERS):
         reach = REACH - 2 * t
         low, high = REACH - reach, REACH + reach + 1
         for a in range(3):
             w4[512 * a + 384 : 512 * a + 512, :] = win[t, a]
-        for i in range(low, high):
-            if t > 0:
-                side_by_side(hf, i)
-                dd[i, 8 : 8 + EXT, :] += dot(x4[i, :, 128:256], head)
-            inputs = lk3[i]
-            for b in range(3):
-                shifted = 0.25 * dd[i, 7 + b : 7 + b + EXT, :]
-                inputs = jnp.where(lane_ext == 32 * b + 8, shifted, inputs)
-            x4[i, :, 384:512] = inputs.astype(BF16)
+        for i in range(low, high) if t > 0 else ():
+            side_by_side(hf, i)
+            dd[i, 8 : 8 + EXT, :] += dot(x4[i, :, 128:256], head)
+            inputs_of(i)
         for first, last in chunks(low + 1, high - 1):
-            count = last - first
+            size = last - first
             if t == 0:
                 in_taps = jnp.concatenate([win[0, a, :, 0:256] for a in range(3)], 0)
                 gates = dot(taps_of(first, last, slice(384, 512)), in_taps)
-                gates = gates.reshape(count, EXT, 256) + part[first:last]
+                gates = gates.reshape(size, EXT, 256) + part[first:last]
             else:
                 gates = dot(taps_of(first, last, slice(0, 512)), w4[:, 0:256])
-                gates = gates.reshape(count, EXT, 256)
+                gates = gates.reshape(size, EXT, 256)
             up[first:last] = jax.nn.sigmoid(gates[:, :, 0:128])
             reset = jax.nn.sigmoid(gates[:, :, 128:256])
             rf[first:last, 8 : 8 + EXT, :] = reset * hf[first:last, 8 : 8 + EXT, :]
         for i in range(low + 1, high - 1):
             side_by_side(rf, i)
         for first, last in chunks(low + 2, high - 2):
-            count = last - first
+            size = last - first
             pre = dot(taps_of(first, last, slice(0, 512)), w4[:, 256:384])
-            candidate = jnp.tanh(pre).reshape(count, EXT, 128)
+            candidate = jnp.tanh(pre).reshape(size, EXT, 128)
             update = up[first:last]
             fresh = (1.0 - update) * hf[first:last, 8 : 8 + EXT, :] + update * candidate
             if t < ITERS - 1:
@@ -538,6 +564,7 @@
             dma((3 * ROWS - 1,)),
             dma((3 * ROWS - 1,)),
             dma((3 * ROWS - 1,)),
+            pltpu.SemaphoreType.REGULAR((3,)),
         ],
         compiler_params=pltpu.CompilerParams(collective_id=0, has_side_effects=True),
         name="stereo",

time: 41.8 us -> 41.5 us (level)
  the two profiles are of different devices: /device:TPU:68 before, /device:TPU:205 now
where the time goes in v3:
time: 41.5 us; the launch traced here: 41.2 us
  Pallas kernels  38.1 us (92%)
  local copies, waits for them, and re-layouts  2.51 us (6%)
  between operations  0.65 us (2%)
    pallas_call x1, Pallas kernels, local(): pl.pallas_call(kernel, out_shape=(jax.ShapeDtypeStruct((1, COLS), F32), j...  38.1 us
    unnamed x4, local copies, waits for them, and re-layouts  2.51 us

profile of v3, /device:TPU:205, one launch (start us, length us, event | category | flops | bytes accessed | tf_op | source)
XLA Modules:
  0.0 41.2 jit_solution(6984557408599733205)
XLA Ops:
  0.6 38.1 %stereo.1 = (f32[1,128]{1,0:T(1,128)}, bf16[128,128]{1,0:T(8,128)(2,1)}) custom-call(f32[8]{0:T(128)} %gain_ref.1, bf16[96,128]{1,0:T(8,128)(2,1)} %bitcast.13, bf16[96,128]{1,0:T(8,128)(2,1)} %bitcast.14, s32[1,128]{1,0:T(1,128)} %lim_in.1, s32[3,1,128]{2,1,0:T(1,128)} %ind_in.1, bf16[128,128]{1,0:T(8,128)(2,1)} %bitcast.11, bf16[216,8]{1,0:T(8,128)(2,1)} %bitcast.10, ...), custom_call_target="tpu_custom_call" | custom-call | tf_op jit(solution)/shard_map/stereo/pallas_call | solution.py:518
  38.7 0.0 copy-start
  38.7 0.6 %copy-done = f32[1,128]{1,0:T(1,128)S(1)} copy-done((f32[1,128]{1,0:T(1,128)S(1)}, f32[1,128]{1,0:T(1,128)}, u32[]{:S(2)}) %copy-start) | copy-done | bytes 536
  39.3 0.5 %copy.14 = f32[1,128]{1,0:T(1,128)} copy(f32[1,128]{1,0:T(1,128)S(1)} %copy-done) | data formatting | bytes 1024
  39.9 1.4 %copy.15 = bf16[1,128,128]{2,1,0:T(8,128)(2,1)} copy(bf16[1,128,128]{2,1,0:T(8,128)(2,1)} %bitcast.12) | data formatting | bytes 65536
Async XLA Ops:
  38.7 0.6 %copy-start = (f32[1,128]{1,0:T(1,128)S(1)}, f32[1,128]{1,0:T(1,128)}, u32[]{:S(2)}) copy-start(f32[1,128]{1,0:T(1,128)} %get-tuple-element.8) | copy-start | bytes 1540

commit v4 on v3

--- a/solution.py
+++ b/solution.py
@@ -44,12 +44,12 @@
 
 
 def kernel(
-    gain_ref, fl_in, fr_in, lim_in, ind_in, h0_in, vk_in, hk_in, ik_in, hw_in,
+    gain_in, fl_in, fr_in, lim_in, ind_in, h0_in, vk_in, hk_in, ik_in, hw_in,
     disp_out, hid_out,
     fl, fr, fp, edge, edge_l, edge_r, lim, ind, vk, ik, hw,
     l3, rt, rg, mean, ins, toep, tw, lg,
     hr, hl, hrt, lm, hf, rf, dd, lk3, x4, up, part, w4, win, ikf,
-    local_sem, feat_send, feat_recv, hid_send, hid_recv, look_send, look_recv, known,
+    local_sem, feat_send, feat_recv, hid_send, hid_recv, look_send, look_recv, known, fin_h, fin_d, gain_ref,
 ):
     band, disp = lax.axis_index("band"), lax.axis_index("disp")
     bands, disps = lax.axis_size("band"), lax.axis_size("disp")
@@ -63,6 +63,7 @@
             [
                 (fl_in, fl.at[1]),
                 (fr_in, fr.at[1]),
+                (gain_in, gain_ref),
                 (vk_in, vk),
                 (ik_in, ik),
                 (hw_in, hw),
@@ -205,6 +206,11 @@
     hids, looks = grouped(hid_make), grouped(look_make)
     order = [0] + [r * side for r in range(1, REACH + 1) for side in (-1, 1)]
 
+    learn(0, 1)
+    tell(1, 2)
+    for r in order[:5]:
+        start(hids, r)
+
     for copy in locals_[2:]:
         copy.wait()
     lane8 = iota((8, COLS), 1)
@@ -224,6 +230,11 @@
             at = (b * 3 + e) * WINDOW
             toep[at : at + WINDOW, :] = jnp.concatenate(rows, 0).astype(BF16)
     tw[...] = dot_nt(eye, toep[...]).astype(BF16)
+
+    learn(1, 2)
+    tell(2, 2)
+    for r in order[5:9]:
+        start(hids, r)
 
     head_rows = jnp.broadcast_to(hw[...].astype(F32), (128, HID)).astype(BF16)
     head = dot_nt(eye, head_rows).astype(BF16)
@@ -327,26 +338,17 @@
         ins[b, 1, 0:16, :] = jnp.concatenate([tail, head8], 0).astype(BF16)
         ins[b, 1, 1024:1040, :] = jnp.concatenate([tail, head8], 0).astype(BF16)
 
-    learn(0, 1)
-    tell(1, 2)
+    learn(2, 2)
+    for r in order[9:]:
+        start(hids, r)
     arrive(feats, 0)
     prepare(1)
     correlate(1)
     for r in (-1, 1):
         arrive(feats, r)
-    for r in order[:5]:
-        start(hids, r)
-    learn(1, 2)
-    tell(2, 2)
-    for r in order[5:9]:
-        start(hids, r)
-    prepare(0)
-    correlate(0)
-    learn(2, 2)
-    for r in order[9:]:
-        start(hids, r)
-    prepare(2)
-    correlate(2)
+    for b in (0, 2):
+        prepare(b)
+        correlate(b)
 
     gain = jnp.zeros((8, COLS), F32)
     for g in range(GROUPS):
@@ -499,8 +501,14 @@
                 hf[REACH, 8 : 8 + EXT, :] = fresh[0].astype(BF16).astype(F32)
         own = hf[REACH, 16 : 16 + COLS, :].astype(BF16)
         disparity += dot_nt(head_row, own)[0:1]
-    hid_out[...] = own
-    disp_out[...] = disparity
+    fin_h[...] = own
+    c1 = pltpu.make_async_copy(fin_h, hid_out, local_sem.at[0])
+    c1.start()
+    fin_d[...] = disparity
+    c2 = pltpu.make_async_copy(fin_d, disp_out, local_sem.at[1])
+    c2.start()
+    c1.wait()
+    c2.wait()
 
     for groups in (feats, hids, looks):
         for r in groups:
@@ -513,7 +521,6 @@
     vol_kernel, group_gain, hid_kernel, in_kernel, head_weight,
 ):
     any_spec = pl.BlockSpec(memory_space=pl.ANY)
-    vmem = pl.BlockSpec(memory_space=pltpu.VMEM)
     dma = pltpu.SemaphoreType.DMA
     disparity, hidden = pl.pallas_call(
         kernel,
@@ -521,8 +528,8 @@
             jax.ShapeDtypeStruct((1, COLS), F32),
             jax.ShapeDtypeStruct((COLS, HID), BF16),
         ),
-        in_specs=[pl.BlockSpec(memory_space=pltpu.SMEM)] + [any_spec] * 9,
-        out_specs=(vmem, vmem),
+        in_specs=[any_spec] * 10,
+        out_specs=(any_spec, any_spec),
         scratch_shapes=[
             pltpu.VMEM((3, CH, COLS), BF16),
             pltpu.VMEM((3, CH, COLS), BF16),
@@ -557,7 +564,7 @@
             pltpu.VMEM((3 * 512, 384), BF16),
             pltpu.VMEM((ITERS, 3, 128, 384), BF16),
             pltpu.VMEM((3, 32, 384), F32),
-            dma((11,)),
+            dma((12,)),
             dma((13,)),
             dma((13,)),
             dma((3 * ROWS - 1,)),
@@ -565,20 +572,28 @@
             dma((3 * ROWS - 1,)),
             dma((3 * ROWS - 1,)),
             pltpu.SemaphoreType.REGULAR((3,)),
+            pltpu.VMEM((COLS, HID), BF16),
+            pltpu.VMEM((1, COLS), F32),
+            pltpu.SMEM((GROUPS,), F32),
         ],
-        compiler_params=pltpu.CompilerParams(collective_id=0, has_side_effects=True),
+        compiler_params=pltpu.CompilerParams(collective_id=0, has_side_effects=True, vmem_limit_bytes=40*2**20),
         name="stereo",
     )(
-        group_gain,
-        feat_left[0],
-        feat_right[0],
-        limit,
-        indices,
-        hidden_start[0],
-        vol_kernel.reshape(216, 8),
-        hid_kernel.reshape(3, 384, 384),
-        in_kernel.transpose(0, 2, 1, 3),
-        head_weight.reshape(1, HID),
+        *[
+            pltpu.with_memory_space_constraint(x, pltpu.HBM)
+            for x in (
+                group_gain,
+                feat_left[0],
+                feat_right[0],
+                limit,
+                indices,
+                hidden_start[0],
+                vol_kernel.reshape(216, 8),
+                hid_kernel.reshape(3, 384, 384),
+                in_kernel.transpose(0, 2, 1, 3),
+                head_weight.reshape(1, HID),
+            )
+        ],
     )
     return disparity, hidden[None]
 

time: 41.5 us -> 37.4 us (0.901)
  the two profiles are of different devices: /device:TPU:205 before, /device:TPU:197 now
where the time goes in v4:
time: 37.4 us; the launch traced here: 37.3 us
  Pallas kernels  35.5 us (95%)
  local copies, waits for them, and re-layouts  1.13 us (3%)
  between operations  0.64 us (2%)
    pallas_call x1, Pallas kernels, local(): pl.pallas_call(kernel, out_shape=(jax.ShapeDtypeStruct((1, COLS), F32), j...  35.5 us
    unnamed x2, local copies, waits for them, and re-layouts  1.13 us

profile of v4, /device:TPU:197, one launch (start us, length us, event | category | flops | bytes accessed | tf_op | source)
XLA Modules:
  0.0 37.3 jit_solution(18365563355190326958)
XLA Ops:
  0.6 35.5 %stereo.1 = (f32[1,128]{1,0:T(1,128)S(1)}, bf16[128,128]{1,0:T(8,128)(2,1)S(1)}) custom-call(f32[8]{0:T(128)} %gain_in.1, bf16[96,128]{1,0:T(8,128)(2,1)} %bitcast.13, bf16[96,128]{1,0:T(8,128)(2,1)} %bitcast.14, s32[1,128]{1,0:T(1,128)} %lim_in.1, s32[3,1,128]{2,1,0:T(1,128)} %ind_in.1, bf16[128,128]{1,0:T(8,128)(2,1)} %bitcast.12, ...), custom_call_target="tpu_custom_call" | custom-call | tf_op jit(solution)/shard_map/stereo/pallas_call | solution.py:525
  36.2 0.5 %copy.14 = f32[1,128]{1,0:T(1,128)} copy(f32[1,128]{1,0:T(1,128)S(1)} %get-tuple-element.8) | data formatting | bytes 1024
  36.7 0.6 %copy.15 = bf16[1,128,128]{2,1,0:T(8,128)(2,1)} copy(bf16[1,128,128]{2,1,0:T(8,128)(2,1)S(1)} %bitcast.8) | data formatting | bytes 65536

commit v5 on v4

--- a/solution.py
+++ b/solution.py
@@ -23,6 +23,7 @@
 BLOCK = 16
 WINDOW = 8 * (BLOCK + 2)
 EXT = COLS + 16
+BOUND = [[BLOCK * blk - e + 1 for e in range(3)] for blk in range(8)]
 LOOK_AT = (0, 16, 24)
 NT = (((1,), (1,)), ((), ()))
 
@@ -266,7 +267,7 @@
     in_group = jnp.where(lane8 // PER_GROUP == iota((8, COLS), 0), 1.0, 0.0)
     lane_ch = iota((CH, COLS), 1)
     eye_ch = one_hot(iota((CH, 128), 0) == iota((CH, 128), 1))
-    apart_block = iota((128, COLS), 1) - iota((128, COLS), 0) // 8
+    pad3 = jnp.zeros((32, 3 * COLS), BF16)
 
     def prepare(b):
         def column(ref, row):
@@ -294,25 +295,25 @@
                     jnp.broadcast_to(rt[side, 2 * k + u : 2 * k + u + 1, :], (8, COLS)) * in_group
                     for u in range(2)
                 ]
-                rg[side, 16 * k : 16 * k + 16, :] = jnp.concatenate(rows, 0).astype(BF16)
+                rg[16 * k : 16 * k + 16, 128 * side : 128 * side + 128] = jnp.concatenate(
+                    rows, 0
+                ).astype(BF16)
         last = jnp.broadcast_to(rt[0, COLS + 1 : COLS + 2, :], (8, COLS)) * in_group
-        rg[0, 8 * COLS : 8 * COLS + 16, :] = jnp.concatenate([last, last], 0).astype(BF16)
+        rg[8 * COLS : 8 * COLS + 16, 0:128] = jnp.concatenate([last, last], 0).astype(BF16)
 
     def correlate(b):
         left3 = l3[b]
-        beyond = dot(rg[0, 8 * COLS : 8 * COLS + 16, 0:CH], left3[:, 256:384])[0:8]
+        beyond = dot(rg[8 * COLS : 8 * COLS + 16, 0:CH], left3[:, 256:384])[0:8]
         tail = [None] * 3
         for blk in range(8):
             rows = slice(128 * blk, 128 * blk + 128)
-            own3 = dot(rg[0, rows, 0:CH], left3)
-            near3 = dot(rg[1, rows, 0:CH], left3) if blk >= 2 else None
+            split = [BOUND[blk][e] for e in range(3)]
+            after = one_hot(jnp.concatenate([lane_ch >= at for at in split], 1))
+            before = one_hot(jnp.concatenate([lane_ch < at for at in split], 1))
+            all3 = dot(rg[rows, :], jnp.concatenate([left3 * after, pad3, left3 * before, pad3], 0))
             for e in range(3):
-                found = own3[:, 128 * e : 128 * e + 128]
+                found = all3[:, 128 * e : 128 * e + 128]
                 first = BLOCK * blk - e + 1
-                if near3 is not None:
-                    found = jnp.where(
-                        apart_block >= first, found, near3[:, 128 * e : 128 * e + 128]
-                    )
                 if blk == 0 and e == 2:
                     found = jnp.concatenate(
                         [jnp.where(lane8 == COLS - 1, beyond, found[0:8]), found[8:]], 0
@@ -358,11 +359,15 @@
         for t in range(ITERS)
     ]
     looked = [jnp.zeros((8, COLS), F32) for _ in range(ITERS)]
+    def window(blk):
+        rows = slice(128 * blk, 128 * blk + WINDOW)
+        return jnp.concatenate([ins[b, e, rows, :] for b in range(3) for e in range(3)], 0)
+
     for blk in range(8):
-        rows = slice(128 * blk, 128 * blk + WINDOW)
-        windows = [ins[b, e, rows, :] for b in range(3) for e in range(3)]
-        conv = dot(tw[...], jnp.concatenate(windows, 0))
-        raw = windows[4].astype(F32)[8:136]
+        if blk % 2 == 0:
+            both = dot(tw[...], jnp.concatenate([window(blk), window(blk + 1)], 1))
+        conv = both[:, 128 * (blk % 2) : 128 * (blk % 2) + 128]
+        raw = ins[1, 1, 128 * blk : 128 * blk + WINDOW, :].astype(F32)[8:136]
         volume = (raw + jnp.maximum(conv, 0.0)).astype(BF16).astype(F32)
         volume = volume.reshape(BLOCK, 8, COLS)
         lg[BLOCK * blk : BLOCK * blk + BLOCK, :] = jnp.sum(volume * gain[None], axis=1)
@@ -385,7 +390,7 @@
     for i, piece in enumerate((high, middle, low)):
         parts = jnp.where(sub8 == i, piece, parts)
     lm[REACH, 1] = jnp.concatenate([looked[0], parts, looked[1], looked[2]], 0).astype(BF16)
-    for r in order:
+    for r in reversed(order):
         start(looks, r)
 
     def side_by_side(ref, i):
@@ -438,8 +443,13 @@
             inputs = jnp.where(lane_ext == 32 * b + 8, shifted, inputs)
         x4[i, :, 384:512] = inputs.astype(BF16)
 
-    for r in order:
-        arrive(looks, r)
+    for groups in (feats, hids):
+        for r in groups:
+            leave(groups, r)
+    for at, r in enumerate(order):
+        if at in (0, 5, 9):
+            for other in order[at : {0: 5, 5: 9, 9: 13}[at]]:
+                arrive(looks, other)
         i = r + REACH
 
         def tile(c, ok):
@@ -463,6 +473,9 @@
         lk3[i] = found
         dd[i, 8 : 8 + EXT, :] = dot(found.astype(BF16), take)
         inputs_of(i)
+
+    for r in looks:
+        leave(looks, r)
 
     for t in range(ITERS):
         reach = REACH - 2 * t
@@ -510,11 +523,6 @@
     c1.wait()
     c2.wait()
 
-    for groups in (feats, hids, looks):
-        for r in groups:
-            if groups[r]:
-                leave(groups, r)
-
 
 def local(
     feat_left, feat_right, limit, indices, hidden_start,
@@ -544,7 +552,7 @@
             pltpu.VMEM((1, HID), BF16),
             pltpu.VMEM((3, CH, 3 * COLS), BF16),
             pltpu.VMEM((2, COLS + 8, COLS), F32),
-            pltpu.VMEM((2, 8 * COLS + 16, COLS), BF16),
+            pltpu.VMEM((8 * COLS + 16, 2 * COLS), BF16),
             pltpu.VMEM((8 * (COLS + 2), COLS), F32),
             pltpu.VMEM((3, 3, 8 * (COLS + 2), COLS), BF16),
             pltpu.VMEM((9 * WINDOW, COLS), BF16),

time: 37.4 us -> 35.2 us (0.941)
  the two profiles are of different devices: /device:TPU:197 before, /device:TPU:385 now
where the time goes in v5:
time: 35.2 us; the launch traced here: 35 us
  Pallas kernels  33.3 us (95%)
  local copies, waits for them, and re-layouts  1.13 us (3%)
  between operations  0.64 us (2%)
    pallas_call x1, Pallas kernels, local(): pl.pallas_call(kernel, out_shape=(jax.ShapeDtypeStruct((1, COLS), F32), j...  33.3 us
    unnamed x2, local copies, waits for them, and re-layouts  1.13 us

profile of v5, /device:TPU:385, one launch (start us, length us, event | category | flops | bytes accessed | tf_op | source)
XLA Modules:
  0.0 35.0 jit_solution(4933114447979927518)
XLA Ops:
  0.6 33.3 %stereo.1 = (f32[1,128]{1,0:T(1,128)S(1)}, bf16[128,128]{1,0:T(8,128)(2,1)S(1)}) custom-call(f32[8]{0:T(128)} %gain_in.1, bf16[96,128]{1,0:T(8,128)(2,1)} %bitcast.13, bf16[96,128]{1,0:T(8,128)(2,1)} %bitcast.14, s32[1,128]{1,0:T(1,128)} %lim_in.1, s32[3,1,128]{2,1,0:T(1,128)} %ind_in.1, bf16[128,128]{1,0:T(8,128)(2,1)} %bitcast.12, ...), custom_call_target="tpu_custom_call" | custom-call | tf_op jit(solution)/shard_map/stereo/pallas_call | solution.py:533
  33.9 0.5 %copy.14 = f32[1,128]{1,0:T(1,128)} copy(f32[1,128]{1,0:T(1,128)S(1)} %get-tuple-element.8) | data formatting | bytes 1024
  34.4 0.6 %copy.15 = bf16[1,128,128]{2,1,0:T(8,128)(2,1)} copy(bf16[1,128,128]{2,1,0:T(8,128)(2,1)S(1)} %bitcast.8) | data formatting | bytes 65536

commit v6 on v5

--- a/solution.py
+++ b/solution.py
@@ -345,9 +345,8 @@
     arrive(feats, 0)
     prepare(1)
     correlate(1)
-    for r in (-1, 1):
-        arrive(feats, r)
     for b in (0, 2):
+        arrive(feats, b - 1)
         prepare(b)
         correlate(b)
 
@@ -446,7 +445,56 @@
     for groups in (feats, hids):
         for r in groups:
             leave(groups, r)
+    def gates_of(t, spans):
+        if t == 0:
+            lanes = slice(384, 512)
+            weights = jnp.concatenate([win[0, a, :, 0:256] for a in range(3)], 0)
+        else:
+            lanes, weights = slice(0, 512), w4[:, 0:256]
+        gates = dot(
+            jnp.concatenate([taps_of(first, last, lanes) for first, last in spans], 0), weights
+        )
+        at = 0
+        for first, last in spans:
+            size = last - first
+            mine = gates[at * EXT : (at + size) * EXT].reshape(size, EXT, 256)
+            if t == 0:
+                mine = mine + part[first:last]
+            up[first:last] = jax.nn.sigmoid(mine[:, :, 0:128])
+            reset = jax.nn.sigmoid(mine[:, :, 128:256])
+            rf[first:last, 8 : 8 + EXT, :] = reset * hf[first:last, 8 : 8 + EXT, :]
+            at += size
+
+    def states_of(t, spans):
+        pre = dot(
+            jnp.concatenate([taps_of(first, last, slice(0, 512)) for first, last in spans], 0),
+            w4[:, 256:384],
+        )
+        at = 0
+        for first, last in spans:
+            size = last - first
+            candidate = jnp.tanh(pre[at * EXT : (at + size) * EXT]).reshape(size, EXT, 128)
+            update = up[first:last]
+            fresh = (1.0 - update) * hf[first:last, 8 : 8 + EXT, :] + update * candidate
+            for i in range(first, last):
+                kept = fresh[i - first]
+                if t < ITERS - 1:
+                    kept = kept * (inside * flag(row_ok[i - REACH]))
+                hf[i, 8 : 8 + EXT, :] = kept.astype(BF16).astype(F32)
+            at += size
+
+    def first_step(gate_spans, state_spans):
+        gates_of(0, gate_spans)
+        for first, last in gate_spans:
+            for i in range(first, last):
+                side_by_side(rf, i)
+        states_of(0, state_spans)
+
+    for a in range(3):
+        w4[512 * a + 384 : 512 * a + 512, :] = win[0, a]
     for at, r in enumerate(order):
+        if at == 9:
+            first_step([(3, 10)], [(4, 9)])
         if at in (0, 5, 9):
             for other in order[at : {0: 5, 5: 9, 9: 13}[at]]:
                 arrive(looks, other)
@@ -477,41 +525,23 @@
     for r in looks:
         leave(looks, r)
 
+    first_step([(1, 3), (10, 12)], [(2, 4), (9, 11)])
     for t in range(ITERS):
         reach = REACH - 2 * t
         low, high = REACH - reach, REACH + reach + 1
-        for a in range(3):
-            w4[512 * a + 384 : 512 * a + 512, :] = win[t, a]
-        for i in range(low, high) if t > 0 else ():
-            side_by_side(hf, i)
-            dd[i, 8 : 8 + EXT, :] += dot(x4[i, :, 128:256], head)
-            inputs_of(i)
-        for first, last in chunks(low + 1, high - 1):
-            size = last - first
-            if t == 0:
-                in_taps = jnp.concatenate([win[0, a, :, 0:256] for a in range(3)], 0)
-                gates = dot(taps_of(first, last, slice(384, 512)), in_taps)
-                gates = gates.reshape(size, EXT, 256) + part[first:last]
-            else:
-                gates = dot(taps_of(first, last, slice(0, 512)), w4[:, 0:256])
-                gates = gates.reshape(size, EXT, 256)
-            up[first:last] = jax.nn.sigmoid(gates[:, :, 0:128])
-            reset = jax.nn.sigmoid(gates[:, :, 128:256])
-            rf[first:last, 8 : 8 + EXT, :] = reset * hf[first:last, 8 : 8 + EXT, :]
-        for i in range(low + 1, high - 1):
-            side_by_side(rf, i)
-        for first, last in chunks(low + 2, high - 2):
-            size = last - first
-            pre = dot(taps_of(first, last, slice(0, 512)), w4[:, 256:384])
-            candidate = jnp.tanh(pre).reshape(size, EXT, 128)
-            update = up[first:last]
-            fresh = (1.0 - update) * hf[first:last, 8 : 8 + EXT, :] + update * candidate
-            if t < ITERS - 1:
-                for i in range(first, last):
-                    kept = fresh[i - first] * (inside * flag(row_ok[i - REACH]))
-                    hf[i, 8 : 8 + EXT, :] = kept.astype(BF16).astype(F32)
-            else:
-                hf[REACH, 8 : 8 + EXT, :] = fresh[0].astype(BF16).astype(F32)
+        if t > 0:
+            for a in range(3):
+                w4[512 * a + 384 : 512 * a + 512, :] = win[t, a]
+            for i in range(low, high):
+                side_by_side(hf, i)
+                dd[i, 8 : 8 + EXT, :] += dot(x4[i, :, 128:256], head)
+                inputs_of(i)
+            for span in chunks(low + 1, high - 1):
+                gates_of(t, [span])
+            for i in range(low + 1, high - 1):
+                side_by_side(rf, i)
+            for span in chunks(low + 2, high - 2):
+                states_of(t, [span])
         own = hf[REACH, 16 : 16 + COLS, :].astype(BF16)
         disparity += dot_nt(head_row, own)[0:1]
     fin_h[...] = own

time: 35.2 us -> 37 us (1.051)
  the two profiles are of different devices: /device:TPU:385 before, /device:TPU:417 now
where the time goes in v6:
time: 37 us; the launch traced here: 36.8 us
  Pallas kernels  35.1 us (95%)
  local copies, waits for them, and re-layouts  1.13 us (3%)
  between operations  0.64 us (2%)
    pallas_call x1, Pallas kernels, local(): pl.pallas_call(kernel, out_shape=(jax.ShapeDtypeStruct((1, COLS), F32), j...  35.1 us
    unnamed x2, local copies, waits for them, and re-layouts  1.13 us

profile of v6, /device:TPU:417, one launch (start us, length us, event | category | flops | bytes accessed | tf_op | source)
XLA Modules:
  0.0 36.8 jit_solution(15217808600069190842)
XLA Ops:
  0.6 35.1 %stereo.1 = (f32[1,128]{1,0:T(1,128)S(1)}, bf16[128,128]{1,0:T(8,128)(2,1)S(1)}) custom-call(f32[8]{0:T(128)} %gain_in.1, bf16[96,128]{1,0:T(8,128)(2,1)} %bitcast.13, bf16[96,128]{1,0:T(8,128)(2,1)} %bitcast.14, s32[1,128]{1,0:T(1,128)} %lim_in.1, s32[3,1,128]{2,1,0:T(1,128)} %ind_in.1, bf16[128,128]{1,0:T(8,128)(2,1)} %bitcast.12, ...), custom_call_target="tpu_custom_call" | custom-call | tf_op jit(solution)/shard_map/stereo/pallas_call | solution.py:563
  35.7 0.5 %copy.14 = f32[1,128]{1,0:T(1,128)} copy(f32[1,128]{1,0:T(1,128)S(1)} %get-tuple-element.8) | data formatting | bytes 1024
  36.2 0.6 %copy.15 = bf16[1,128,128]{2,1,0:T(8,128)(2,1)} copy(bf16[1,128,128]{2,1,0:T(8,128)(2,1)S(1)} %bitcast.8) | data formatting | bytes 65536
